TPU v7x, 512 devices: a whole 4x4x16 slice. The times are simulated.
512 devices in a mesh: win: 64 (over y, z), state: 8 (over x, core).
Axes of the slice: x: 4, y: 4, z: 16, core: 2. Of those that a mesh axis runs over, the one named last changes fastest.
Arguments:
- anomalies: float32 [64, 2048, 256], P('win', 'state'), may hold values from -12 to 12
- mean_state: float32 [64, 2048], P('win', 'state'), may hold values from -6 to 6
- obs_rows: int32 [64, 1024], P('win', 'state'), may hold values from 0 to 255
- obs_precision: float32 [64, 1024], P('win', 'state'), may hold values from 0.001953125 to 0.01953125
Outputs:
- updated: float32 [64, 2048, 256], P('win', 'state')
Inputs may be any that keep to these rules, and one draw needn't show every extreme that they name: Observation j of window w reads state row (j // 128) * 256 + obs_rows[w, j], a row of the same block of 256 rows.
All inputs are finite; a program needn't handle non-finite values.
Results may differ from a plain program's by a relative error of at most 0.0003.
Values sent between devices are 32-bit elements; how exact they have to be, the bound alone decides.
No kernel may reach another device: no remote copies, remote signals or barrier semaphores. Data moves between devices by JAX's collectives and lax.ppermute only.
A program may use at most 128 MiB of HBM per device.

v0:
```python
import jax
import jax.numpy as jnp
from jax import lax
from jax.sharding import PartitionSpec as P

NS_STEPS = 3


PRECISE = lax.Precision.HIGHEST


def carried_in(value, axis, join, neutral):
    count, mine = (lax.axis_size(axis), lax.axis_index(axis))
    pieces = lax.all_gather(value, axis)
    pieces = pieces[::-1]
    mine = count - 1 - mine
    running = jnp.full_like(value, 0) + jnp.asarray(neutral, value.dtype)

    def step(position, running):
        longer = join(running, pieces[position])
        return jnp.where(position < mine, longer, running)

    return lax.fori_loop(0, count - 1, step, running)


def high_dot(left, right):
    return jnp.dot(left, right, precision=PRECISE, preferred_element_type=jnp.float32)


def inverse_root(gram_matrix):
    members = gram_matrix.shape[0]
    unit_matrix = jnp.eye(members, dtype=jnp.float32)
    system = unit_matrix + gram_matrix
    frob_scale = jnp.sqrt(jnp.sum(system * system))
    root_iter = system / frob_scale
    factor = 1.5 * unit_matrix - 0.5 * root_iter
    inverse = factor
    root_iter = high_dot(root_iter, factor)
    for ns_index in range(1, NS_STEPS):
        factor = 1.5 * unit_matrix - 0.5 * high_dot(inverse, root_iter)
        if ns_index + 1 < NS_STEPS:
            root_iter = high_dot(root_iter, factor)
        inverse = high_dot(factor, inverse)
    return inverse * (members / jnp.trace(inverse))


def gram_terms(current, mean_state, obs_rows, obs_precision):
    row_count = current.shape[1]
    members = current.shape[2]
    positions = jnp.arange(row_count, dtype=jnp.int32)
    selector = (obs_rows[:, :, None] == positions[None, None, :]).astype(jnp.float32)
    picked = jnp.einsum("wor,wrm->wom", selector, current, precision=PRECISE)
    base_value = jnp.einsum("wor,wr->wo", selector, mean_state, precision=PRECISE)
    predicted = jnp.tanh(base_value[:, :, None] + picked)
    centred = (predicted - jnp.mean(predicted, axis=2, keepdims=True)) * jnp.sqrt(obs_precision)[
        :, :, None
    ]
    return jnp.einsum("wom,won->wmn", centred, centred, precision=PRECISE) / (members - 1)


def combine_later(earlier, later_part):
    return high_dot(later_part, earlier)


def shards(anomalies, mean_state, obs_rows, obs_precision):
    current = anomalies
    window_count = anomalies.shape[0]
    members = anomalies.shape[2]
    unit_matrix = jnp.eye(members, dtype=jnp.float32)
    local_grams = gram_terms(current, mean_state, obs_rows, obs_precision)
    summed = lax.psum(local_grams, "state")
    transforms = [inverse_root(summed[0])]
    running = transforms[window_count - 1]
    later_product = carried_in(running, "win", combine_later, unit_matrix)
    current = jnp.stack([high_dot(current[0], high_dot(running, later_product))])
    return current


def solution(mesh):
    placed = (P("win", "state", None), P("win", "state"), P("win", "state"), P("win", "state"))
    return jax.shard_map(
        shards, mesh=mesh, in_specs=placed, out_specs=P("win", "state", None), check_vma=False
    )
```

profile of v0, /device:TPU:1, one launch (start us, length us, event | category | flops | bytes accessed | tf_op | source)
XLA Modules:
  0.0 400.5 jit_solution(16687633099318122900)
XLA Ops:
  10.5 79.7 %all-reduce.2.cloned.1.call-done = f32[1,256,256]{2,1,0:T(8,128)} async-done(((f32[1,256,256]{2,1,0:T(8,128)}), f32[1,256,256]{2,1,0:T(8,128)}) %all-reduce.2.cloned.1.call-update) | async-done | bytes 262160 | tf_op jit(solution)/shard_map/psum | solution.py:71
  90.2 1.6 multiply_reduce_fusion
  92.5 1.5 fusion.7
  93.9 1.4 fusion.4
  95.7 1.4 fusion.32
  99.9 192.8 %all-gather.3.cloned.1.call-done = f32[16384,256]{1,0:T(8,128)} async-done(((f32[256,256]{1,0:T(8,128)}), f32[16384,256]{1,0:T(8,128)}) %all-gather.3.cloned.1.call-update) | async-done | bytes 16777232 | tf_op jit(solution)/shard_map/all_gather | solution.py:14
  292.8 11.5 %rev.3 = f32[64,256,256]{2,1,0:T(8,128)} reverse(f32[64,256,256]{2,1,0:T(8,128)} %bitcast.62), dimensions={0} | reverse | bytes 33554432 | tf_op jit(solution)/shard_map/rev | solution.py:15
  304.3 87.5 %while.13 = (s32[]{:T(128)}, f32[256,256]{1,0:T(8,128)S(1)}, s32[]{:T(128)}, f32[64,256,256]{2,1,0:T(8,128)}, s32[]{:T(128)}) while((s32[]{:T(128)}, f32[256,256]{1,0:T(8,128)S(1)}, s32[]{:T(128)}, f32[64,256,256]{2,1,0:T(8,128)}, s32[]{:T(128)}) %tuple.30), condition=%wide.region_5.6_spmd, body=%wide.region_4.5_spmd.sunk | while | flops 201392128 | bytes 1573447 | solution.py:23
  305.7 1.3 convolution_select_fusion.2
  307.1 1.3 convolution_select_fusion.2
  308.4 1.3 convolution_select_fusion.2
  309.8 1.3 convolution_select_fusion.2
  311.2 1.3 convolution_select_fusion.2
  314.0 1.3 convolution_select_fusion.2
  315.4 1.3 convolution_select_fusion.2
  318.2 1.3 convolution_select_fusion.2
  319.6 1.3 convolution_select_fusion.2
  322.3 1.3 convolution_select_fusion.2
  323.7 1.3 convolution_select_fusion.2
  325.1 1.3 convolution_select_fusion.2
  326.5 1.3 convolution_select_fusion.2
  327.9 1.3 convolution_select_fusion.2
  329.3 1.3 convolution_select_fusion.2
  330.7 1.3 convolution_select_fusion.2
  332.1 1.3 convolution_select_fusion.2
  333.5 1.3 convolution_select_fusion.2
  334.8 1.3 convolution_select_fusion.2
  336.2 1.3 convolution_select_fusion.2
  337.6 1.3 convolution_select_fusion.2
  340.4 1.3 convolution_select_fusion.2
  341.8 1.3 convolution_select_fusion.2
  344.6 1.3 convolution_select_fusion.2
  346.0 1.3 convolution_select_fusion.2
  348.7 1.3 convolution_select_fusion.2
  350.1 1.3 convolution_select_fusion.2
  351.5 1.3 convolution_select_fusion.2
  352.9 1.3 convolution_select_fusion.2
  354.3 1.3 convolution_select_fusion.2
  355.7 1.3 convolution_select_fusion.2
  357.1 1.3 convolution_select_fusion.2
  358.5 1.3 convolution_select_fusion.2
  359.9 1.3 convolution_select_fusion.2
  361.2 1.3 convolution_select_fusion.2
  362.6 1.3 convolution_select_fusion.2
  364.0 1.3 convolution_select_fusion.2
  366.8 1.3 convolution_select_fusion.2
  368.2 1.3 convolution_select_fusion.2
  371.0 1.3 convolution_select_fusion.2
  (107 shorter events, 40.1 us)
Async XLA Ops:
  6.5 1.0 copy-start
  6.5 83.6 %all-reduce.2.cloned.1.call-start = ((), (), s32[]{:S(2)}) async-start(), calls=%async_computation | async-start | bytes 524288 | tf_op jit(solution)/shard_map/psum | solution.py:71
  10.4 282.3 %all-gather.3.cloned.1.call-start = ((), (), s32[]{:S(2)}) async-start(), calls=%async_computation.1 | async-start | bytes 17039360 | tf_op jit(solution)/shard_map/all_gather | solution.py:14
  292.8 99.0 %copy-start.1 = (f32[256,256]{1,0:T(8,128)S(1)}, f32[256,256]{1,0:T(8,128)}, u32[]{:S(2)}) copy-start(f32[256,256]{1,0:T(8,128)} %broadcast_multiply_fusion) | copy-start | bytes 786436
Sparse Core Ops, SparseCore 0:
  10.6 79.5 all-reduce.1
  100.0 192.7 all-gather.2
where the time goes:
time: 403 us; the launch traced here: 400 us
  waiting for transfers between devices  273 us (68%)
  matrix products  94.2 us (23%)
  between operations  14.9 us (4%)
  local copies, waits for them, and re-layouts  14.2 us (4%)
    all_gather x1, waiting for transfers between devices, carried_in(): pieces = lax.all_gather(value, axis)  193 us
    dot_general x71, matrix products, high_dot(): jnp.dot(left, right, precision=PRECISE, preferred_element_type=jnp.float32)  91 us
    psum x1, waiting for transfers between devices, shards(): summed = lax.psum(local_grams, 'state')  79.7 us
    rev x1, local copies, waits for them, and re-layouts, carried_in(): pieces = pieces[::-1]  11.5 us
  transfers between devices with their start and end apart: 2, of which 2 were waited for; matrix products, arithmetic and copies ran while one was open for 0% of the time, Pallas kernels for 0%

commit v1 on v0

v1 whole, which is shorter than its diff:
```python
import functools

import jax
import jax.numpy as jnp
from jax import lax
from jax.experimental import pallas as pl
from jax.experimental.pallas import tpu as pltpu
from jax.sharding import Mesh, PartitionSpec as P

F32 = jnp.float32
BF16 = jnp.bfloat16
N = 256
H = 128
PACK = 272
NS_STEPS = 3


def split(a):
    hi = a.astype(BF16)
    lo = (a - hi.astype(F32)).astype(BF16)
    return hi, lo


def mm(a, b):
    dot = functools.partial(jnp.dot, preferred_element_type=F32)
    return dot(a[0], b[0]) + (dot(a[0], b[1]) + dot(a[1], b[0]))


def eye_mask(n):
    i = lax.broadcasted_iota(jnp.int32, (n, n), 0)
    j = lax.broadcasted_iota(jnp.int32, (n, n), 1)
    return i, j


def column(row, n):
    i, j = eye_mask(n)
    return jnp.sum(jnp.where(i == j, row, 0.0), axis=1, keepdims=True)


def pack(m, out, copies):
    i, j = eye_mask(H)
    first, corner = m[:H, :H], m[H:, H:]
    rows = jnp.where(i <= j, first, corner)
    diag = jnp.sum(jnp.where(i == j, corner, 0.0), axis=0, keepdims=True)
    tail = jnp.where(lax.broadcasted_iota(jnp.int32, (PACK - N, H), 0) == 0, diag, 0.0)
    out[:H, :] = rows
    out[H:N, :] = m[:H, H:]
    out[N:, :] = tail


def unpack(p):
    i, j = eye_mask(H)
    rows, cross, diag = p[:H], p[H:N], p[N:N + 1]
    turned = rows.T
    first = jnp.where(i <= j, rows, turned)
    corner = jnp.where(i > j, rows, jnp.where(i < j, turned, diag))
    top = jnp.concatenate([first, cross], axis=1)
    low = jnp.concatenate([cross.T, corner], axis=1)
    return jnp.concatenate([top, low], axis=0)


def gram_kernel(cur_ref, mean_ref, rows_ref, prec_ref, out_ref):
    value = cur_ref[...] + column(mean_ref[...], N)
    state_row = lax.broadcasted_iota(jnp.int32, (N, H), 0)
    chosen = (state_row == rows_ref[...]).astype(F32).T.astype(BF16)
    dot = functools.partial(jnp.dot, preferred_element_type=F32)
    one = value.astype(BF16)
    rest = value - one.astype(F32)
    two = rest.astype(BF16)
    three = (rest - two.astype(F32)).astype(BF16)
    picked = dot(chosen, one) + (dot(chosen, two) + dot(chosen, three))
    predicted = jnp.tanh(picked)
    centred = predicted - jnp.mean(predicted, axis=1, keepdims=True)
    centred = centred * jnp.sqrt(column(prec_ref[...], H))
    gram = mm(split(centred.T), split(centred)) * (1.0 / (N - 1))
    pack(gram, out_ref, 1)


def root_kernel(parts_ref, out_ref, packed):
    total = (parts_ref[0] + parts_ref[1]) + (parts_ref[2] + parts_ref[3])
    i, j = eye_mask(N)
    unit = jnp.where(i == j, 1.0, 0.0)
    system = unpack(total) + unit
    square = jnp.sum(jnp.sum(system * system, axis=0, keepdims=True), axis=1, keepdims=True)
    root = system * (1.0 / jnp.sqrt(square))
    factor = 1.5 * unit - 0.5 * root
    inverse = split(factor)
    root = split(mm(split(root), inverse))
    for step in range(1, NS_STEPS):
        factor = split(1.5 * unit - 0.5 * mm(inverse, root))
        if step + 1 < NS_STEPS:
            root = split(mm(root, factor))
        last = mm(factor, inverse)
        inverse = split(last)
    diag = jnp.where(i == j, last, 0.0)
    trace = jnp.sum(jnp.sum(diag, axis=0, keepdims=True), axis=1, keepdims=True)
    pack(last * (N / trace), packed, 1)
    core = lax.axis_index("core")
    half = packed[pl.ds(pl.multiple_of(core * (PACK // 2), 8), PACK // 2), :]
    for copy in range(4):
        out_ref[copy] = half


def transforms(parts_ref):
    out = []
    for place in range(4):
        out.append(unpack(jnp.concatenate([parts_ref[0, place], parts_ref[1, place]], axis=0)))
    return out


def half_of(total, half_ref):
    core = lax.axis_index("core")

    @pl.when(core == 0)
    def _():
        half_ref[...] = total[:H]

    @pl.when(core == 1)
    def _():
        half_ref[...] = total[H:]


def quad_kernel(parts_ref, total_ref, half_ref):
    one, two, three, four = [split(t) for t in transforms(parts_ref)]
    total = mm(split(mm(one, two)), split(mm(three, four)))
    total_ref[...] = total
    half_of(total, half_ref)


def quad_apply_kernel(parts_ref, cur_ref, out_ref):
    mine = lax.axis_index("zl")
    out_ref[...] = cur_ref[...]
    for place in range(4):

        @pl.when(place >= mine)
        def _():
            t = unpack(jnp.concatenate([parts_ref[0, place], parts_ref[1, place]], axis=0))
            out_ref[...] = mm(split(out_ref[...]), split(t))


def pair_kernel(first_of, copies, mine_ref, other_ref, total_ref, half_ref):
    first = first_of(lax.axis_index("zh"))

    @pl.when(first)
    def _():
        total_ref[...] = mm(split(mine_ref[...]), split(other_ref[...]))

    @pl.when(jnp.logical_not(first))
    def _():
        total_ref[...] = mm(split(other_ref[...]), split(mine_ref[...]))

    core = lax.axis_index("core")
    half = total_ref[pl.ds(pl.multiple_of(core * H, 8), H), :]
    if copies:
        for copy in range(copies):
            half_ref[copy] = half
    else:
        half_ref[...] = half


def pair_apply_kernel(first_of, other_ref, cur_ref, out_ref):
    first = first_of(lax.axis_index("zh"))

    @pl.when(first)
    def _():
        out_ref[...] = mm(split(cur_ref[...]), split(other_ref[...]))

    @pl.when(jnp.logical_not(first))
    def _():
        out_ref[...] = cur_ref[...]


def row_apply_kernel(parts_ref, cur_ref, out_ref):
    mine = lax.axis_index("y")
    out_ref[...] = cur_ref[...]
    for place in range(1, 4):

        @pl.when(place > mine)
        def _():
            t = jnp.concatenate([parts_ref[0, place], parts_ref[1, place]], axis=0)
            out_ref[...] = mm(split(out_ref[...]), split(t))


VMEM = pl.BlockSpec(memory_space=pltpu.VMEM)


def call(kernel, name, outs, args, products, scratch=()):
    many = isinstance(outs, list)
    shapes = [jax.ShapeDtypeStruct(s, F32) for s in (outs if many else [outs])]
    moved = sum(a.size * 4 for a in args) + sum(s.size * 4 for s in shapes)
    return pl.pallas_call(
        kernel,
        name=name,
        out_shape=shapes if many else shapes[0],
        in_specs=[VMEM] * len(args),
        out_specs=[VMEM] * len(shapes) if many else VMEM,
        scratch_shapes=list(scratch),
        cost_estimate=pl.CostEstimate(
            flops=products * 6 * N * N * N, bytes_accessed=moved, transcendentals=0
        ),
    )(*args)


def in_left_quad(quad):
    return quad % 2 == 0


def in_left_half(quad):
    return quad < 2


PAIR_ONE = [(quad, quad ^ 1) for quad in range(4)]
PAIR_TWO = [(quad, quad ^ 3) for quad in range(4)]


def shards(anomalies, mean_state, obs_rows, obs_precision):
    current = anomalies[0]
    gram = call(gram_kernel, "gram", (PACK, H), (current, mean_state, obs_rows, obs_precision), 1)
    both = lax.all_gather(gram, "core")
    spread = jnp.broadcast_to(both[0] + both[1], (4, PACK, H))
    parts = lax.all_to_all(spread, "x", 0, 0)
    half = call(
        root_kernel, "root", (4, PACK // 2, H), (parts,), 6, [pltpu.VMEM((PACK, H), F32)]
    )
    parts = lax.all_gather(lax.all_to_all(half, "zl", 0, 0), "core")
    full = (N, N)
    total, half = call(quad_kernel, "quad", [full, (H, N)], (parts,), 3)
    current = call(quad_apply_kernel, "quad_apply", full, (parts, current), 4)
    for pairs, first_of, copies in ((PAIR_ONE, in_left_quad, 0), (PAIR_TWO, in_left_half, 4)):
        other = lax.ppermute(half, "zh", pairs)
        other = lax.all_gather(other, "core", tiled=True)
        half_shape = (copies, H, N) if copies else (H, N)
        total, half = call(
            functools.partial(pair_kernel, first_of, copies),
            "pair",
            [full, half_shape],
            (total, other),
            1,
        )
        current = call(
            functools.partial(pair_apply_kernel, first_of), "pair_apply", full, (other, current), 1
        )
    parts = lax.all_gather(lax.all_to_all(half, "y", 0, 0), "core")
    return call(row_apply_kernel, "row_apply", full, (parts, current), 3)[None]


def solution(mesh):
    devices = mesh.devices.reshape(4, 4, 4, 4, 2)
    grid = Mesh(devices, ("y", "zh", "zl", "x", "core"))
    win, state = ("y", "zh", "zl"), ("x", "core")
    placed = (P(win, state, None), P(win, state), P(win, state), P(win, state))
    return jax.shard_map(
        shards, mesh=grid, in_specs=placed, out_specs=P(win, state, None), check_vma=False
    )
```

time: 403 us -> 135 us (0.33)
  waiting for transfers between devices: 273 us -> 32 us
  matrix products: 94.2 us -> 0 us
  blocking collectives: 0 us -> 54.1 us
  Pallas kernels: 0 us -> 23.2 us
  local copies, waits for them, and re-layouts: 14.2 us -> 0.04 us
  starting transfers between devices: 0.04 us -> 11.3 us
    all_gather x1, waiting for transfers between devices: 193 us -> 9.16 us  [shards(): parts = lax.all_gather(lax.all_to_all(half, 'y', 0, 0), 'core')]
    dot_general x74 -> x0, matrix products: 94.2 us -> none  [the longest x71 91 us: high_dot(): jnp.dot(left, right, precision=PRECISE, preferred_element_type=jnp.float32)]
    psum x1 -> x0, waiting for transfers between devices: 79.7 us -> none  [shards(): summed = lax.psum(local_grams, 'state')]
    all_to_all x0 -> x3, blocking collectives: none -> 36.1 us  [the longest x1 12.9 us: shards(): parts = lax.all_gather(lax.all_to_all(half, 'y', 0, 0), 'core')]
    pallas_call x0 -> x9, Pallas kernels: none -> 23.2 us  [call(): pl.pallas_call(kernel, name=name, out_shape=shapes if many else shapes[0]...]
    ppermute x0 -> x2, waiting for transfers between devices: none -> 22.8 us  [shards(): other = lax.ppermute(half, 'zh', pairs)]
    all_gather x0 -> x4, blocking collectives: none -> 18.1 us  [the longest x1 8.68 us: shards(): both = lax.all_gather(gram, 'core')]
    rev x1 -> x0, local copies, waits for them, and re-layouts: 11.5 us -> none  [carried_in(): pieces = pieces[::-1]]
  transfers between devices with their start and end apart: 2 -> 3, of which waited for: 2 -> 3; matrix products, arithmetic and copies ran while one was open for 0% -> 0% of each run, Pallas kernels for 0% -> 5%
where the time goes in v1:
time: 135 us; the launch traced here: 134 us
  blocking collectives  54.1 us (40%)
  waiting for transfers between devices  32 us (24%)
  Pallas kernels  23.2 us (17%)
  between operations  13.4 us (10%)
  starting transfers between devices  11.3 us (8%)
    pallas_call x9, Pallas kernels, call(): pl.pallas_call(kernel, name=name, out_shape=shapes if many else shapes[0]...  23.2 us
    ppermute x2, waiting for transfers between devices, shards(): other = lax.ppermute(half, 'zh', pairs)  22.8 us
    all_to_all x1, blocking collectives, shards(): parts = lax.all_gather(lax.all_to_all(half, 'y', 0, 0), 'core')  12.9 us
    all_to_all x1, blocking collectives, shards(): parts = lax.all_to_all(spread, 'x', 0, 0)  12.5 us
    ppermute x2, starting transfers between devices, shards(): other = lax.ppermute(half, 'zh', pairs)  11.3 us
    all_to_all x1, blocking collectives, shards(): parts = lax.all_gather(lax.all_to_all(half, 'zl', 0, 0), 'core')  10.6 us
    all_gather x1, waiting for transfers between devices, shards(): parts = lax.all_gather(lax.all_to_all(half, 'y', 0, 0), 'core')  9.16 us
    all_gather x1, blocking collectives, shards(): both = lax.all_gather(gram, 'core')  8.68 us
  transfers between devices with their start and end apart: 3, of which 3 were waited for; matrix products, arithmetic and copies ran while one was open for 0% of the time, Pallas kernels for 5%

profile of v1, /device:TPU:1, one launch (start us, length us, event | category | flops | bytes accessed | tf_op | source)
XLA Modules:
  0.0 134.1 jit_solution(16394257338472637786)
XLA Ops:
  6.5 0.0 all-gather.5.cloned.1.call-start
  6.5 2.4 %gram.1 = f32[272,128]{1,0:T(8,128)} custom-call(f32[256,256]{1,0:T(8,128)} %bitcast.7, f32[1,256]{1,0:T(1,128)} %mean_ref.1, s32[1,128]{1,0:T(1,128)} %rows_ref.1, f32[1,128]{1,0:T(1,128)} %prec_ref.1), custom_call_target="tpu_custom_call" | custom-call | flops 100663296 | bytes 403456 | tf_op jit(solution)/shard_map/gram/pallas_call | solution.py:191
  9.0 8.7 %all-gather = f32[544,128]{1,0:T(8,128)S(1)} all-gather(f32[272,128]{1,0:T(8,128)} %gram.1), channel_id=2, replica_groups=mesh['y'=4,'zh'=4,'zl'=4,'x'=4,'core'=2] {'core'}, dimensions={0}, use_global_device_ids=true | all-gather | bytes 417792 | tf_op jit(solution)/shard_map/all_gather | solution.py:219
  17.7 12.5 %all_to_all.15.parts_ref = f32[4,272,128]{2,1,0:T(8,128)} all-to-all(f32[4,272,128]{2,1,0:T(8,128)S(1)} %broadcast_in_dim.6), channel_id=1, replica_groups=mesh['y'=4,'zh'=4,'zl'=4,'x'=4,'core'=2] {'x'}, dimensions={0} | all-to-all | bytes 1114112 | tf_op jit(solution)/shard_map/all_to_all | solution.py:221
  30.3 3.7 %root.1 = f32[4,136,128]{2,1,0:T(8,128)} custom-call(f32[4,272,128]{2,1,0:T(8,128)} %all_to_all.15.parts_ref), custom_call_target="tpu_custom_call" | custom-call | flops 603979776 | bytes 835584 | tf_op jit(solution)/shard_map/root/pallas_call | solution.py:191
  34.0 10.6 %all_to_all.16 = f32[4,136,128]{2,1,0:T(8,128)S(1)} all-to-all(f32[4,136,128]{2,1,0:T(8,128)} %root.1), channel_id=1, replica_groups=mesh['y'=4,'zh'=4,'zl'=4,'x'=4,'core'=2] {'zl'}, dimensions={0} | all-to-all | bytes 557056 | tf_op jit(solution)/shard_map/all_to_all | solution.py:225
  44.6 4.9 %all-gather.1 = f32[8,136,128]{2,1,0:T(8,128)} all-gather(f32[4,136,128]{2,1,0:T(8,128)S(1)} %all_to_all.16), channel_id=3, replica_groups=mesh['y'=4,'zh'=4,'zl'=4,'x'=4,'core'=2] {'core'}, dimensions={0}, use_global_device_ids=true | all-gather | bytes 835584 | tf_op jit(solution)/shard_map/all_gather | solution.py:225
  49.5 2.7 %quad.1 = (f32[256,256]{1,0:T(8,128)}, f32[128,256]{1,0:T(8,128)}) custom-call(f32[2,4,136,128]{3,2,1,0:T(8,128)} %bitcast.5), custom_call_target="tpu_custom_call" | custom-call | flops 301989888 | bytes 950272 | tf_op jit(solution)/shard_map/quad/pallas_call | solution.py:191
  52.2 6.3 %collective-permute-start = (f32[128,256]{1,0:T(8,128)}, f32[128,256]{1,0:T(8,128)S(1)}, u32[]{:S(2)}, u32[]{:S(2)}) collective-permute-start(f32[128,256]{1,0:T(8,128)} %get-tuple-element.11), channel_id=1, source_target_pairs={{0,32},{32,0},{64,96},{96,64},{1,33},{33,1},{65,97},{97,65},{2,34}... | collective-permute-start | bytes 393224 | tf_op jit(solution)/shard_map/ppermute | solution.py:230
  58.5 13.5 %collective-permute-done = f32[128,256]{1,0:T(8,128)S(1)} collective-permute-done((f32[128,256]{1,0:T(8,128)}, f32[128,256]{1,0:T(8,128)S(1)}, u32[]{:S(2)}, u32[]{:S(2)}) %collective-permute-start) | collective-permute-done | bytes 131104 | tf_op jit(solution)/shard_map/ppermute | solution.py:230
  72.0 2.2 %all_gather.28.other_ref = f32[256,256]{1,0:T(8,128)} all-gather(f32[128,256]{1,0:T(8,128)S(1)} %collective-permute-done), channel_id=1, replica_groups=mesh['y'=4,'zh'=4,'zl'=4,'x'=4,'core'=2] {'core'}, dimensions={0}, use_global_device_ids=true | all-gather | bytes 393216 | tf_op jit(solution)/shard_map/all_gather | solution.py:231
  74.2 2.1 %pair.2 = (f32[256,256]{1,0:T(8,128)}, f32[128,256]{1,0:T(8,128)}) custom-call(f32[256,256]{1,0:T(8,128)} %get-tuple-element.10.mine_ref, f32[256,256]{1,0:T(8,128)} %all_gather.28.other_ref), custom_call_target="tpu_custom_call" | custom-call | flops 100663296 | bytes 917504 | tf_op jit(solution)/shard_map/pair/pallas_call | solution.py:191
  76.3 5.0 %collective-permute-start.1 = (f32[128,256]{1,0:T(8,128)}, f32[128,256]{1,0:T(8,128)S(1)}, u32[]{:S(2)}, u32[]{:S(2)}) collective-permute-start(f32[128,256]{1,0:T(8,128)} %get-tuple-element.13), channel_id=1, source_target_pairs={{0,96},{32,64},{64,32},{96,0},{1,97},{33,65},{65,33},{97,1},{2,98}... | collective-permute-start | bytes 393224 | tf_op jit(solution)/shard_map/ppermute | solution.py:230
  81.3 9.3 %collective-permute-done.1 = f32[128,256]{1,0:T(8,128)S(1)} collective-permute-done((f32[128,256]{1,0:T(8,128)}, f32[128,256]{1,0:T(8,128)S(1)}, u32[]{:S(2)}, u32[]{:S(2)}) %collective-permute-start.1) | collective-permute-done | bytes 131104 | tf_op jit(solution)/shard_map/ppermute | solution.py:230
  90.6 2.2 %all_gather.29.other_ref = f32[256,256]{1,0:T(8,128)} all-gather(f32[128,256]{1,0:T(8,128)S(1)} %collective-permute-done.1), channel_id=1, replica_groups=mesh['y'=4,'zh'=4,'zl'=4,'x'=4,'core'=2] {'core'}, dimensions={0}, use_global_device_ids=true | all-gather | bytes 393216 | tf_op jit(solution)/shard_map/all_gather | solution.py:231
  92.8 2.2 %pair.3 = (f32[256,256]{1,0:T(8,128)}, f32[4,128,256]{2,1,0:T(8,128)}) custom-call(f32[256,256]{1,0:T(8,128)} %get-tuple-element.12.mine_ref, f32[256,256]{1,0:T(8,128)} %all_gather.29.other_ref), custom_call_target="tpu_custom_call" | custom-call | flops 100663296 | bytes 1310720 | tf_op jit(solution)/shard_map/pair/pallas_call | solution.py:191
  95.0 12.9 %all_to_all.17 = f32[4,128,256]{2,1,0:T(8,128)} all-to-all(f32[4,128,256]{2,1,0:T(8,128)} %get-tuple-element.14), channel_id=1, replica_groups=mesh['y'=4,'zh'=4,'zl'=4,'x'=4,'core'=2] {'y'}, dimensions={0} | all-to-all | bytes 1048576 | tf_op jit(solution)/shard_map/all_to_all | solution.py:243
  108.0 0.0 all-gather.5.cloned.1.call-update
  108.0 3.3 %quad_apply.1.cur_ref = f32[256,256]{1,0:T(8,128)} custom-call(f32[2,4,136,128]{3,2,1,0:T(8,128)} %bitcast.6, f32[256,256]{1,0:T(8,128)} %bitcast.8), custom_call_target="tpu_custom_call" | custom-call | flops 402653184 | bytes 1081344 | tf_op jit(solution)/shard_map/quad_apply/pallas_call | solution.py:191
  111.3 2.0 %pair_apply.2.cur_ref = f32[256,256]{1,0:T(8,128)} custom-call(f32[256,256]{1,0:T(8,128)} %all_gather.28.other_ref, f32[256,256]{1,0:T(8,128)} %quad_apply.1.cur_ref), custom_call_target="tpu_custom_call" | custom-call | flops 100663296 | bytes 786432 | tf_op jit(solution)/shard_map/pair_apply/pallas_call | solution.py:191
  113.3 2.0 %pair_apply.3.cur_ref = f32[256,256]{1,0:T(8,128)} custom-call(f32[256,256]{1,0:T(8,128)} %all_gather.29.other_ref, f32[256,256]{1,0:T(8,128)} %pair_apply.2.cur_ref), custom_call_target="tpu_custom_call" | custom-call | flops 100663296 | bytes 786432 | tf_op jit(solution)/shard_map/pair_apply/pallas_call | solution.py:191
  115.3 9.2 %all-gather.5.cloned.1.call-done = f32[8,128,256]{2,1,0:T(8,128)} async-done(((f32[4,128,256]{2,1,0:T(8,128)}), f32[8,128,256]{2,1,0:T(8,128)}) %all-gather.5.cloned.1.call-update) | async-done | bytes 1048592 | tf_op jit(solution)/shard_map/all_gather | solution.py:243
  124.4 2.8 %row_apply.1 = f32[256,256]{1,0:T(8,128)} custom-call(f32[2,4,128,256]{3,2,1,0:T(8,128)} %bitcast.4, f32[256,256]{1,0:T(8,128)} %pair_apply.3.cur_ref), custom_call_target="tpu_custom_call" | custom-call | flops 301989888 | bytes 1572864 | tf_op jit(solution)/shard_map/row_apply/pallas_call | solution.py:191
  (2 shorter events, 0.1 us)
Async XLA Ops:
  6.5 117.9 %all-gather.5.cloned.1.call-start = ((), (), s32[]{:S(2)}) async-start(), calls=%async_computation.3 | async-start | bytes 1572864 | tf_op jit(solution)/shard_map/all_gather | solution.py:243
  52.2 19.8 %collective-permute-start = (f32[128,256]{1,0:T(8,128)}, f32[128,256]{1,0:T(8,128)S(1)}, u32[]{:S(2)}, u32[]{:S(2)}) collective-permute-start(f32[128,256]{1,0:T(8,128)} %get-tuple-element.11), channel_id=1, source_target_pairs={{0,32},{32,0},{64,96},{96,64},{1,33},{33,1},{65,97},{97,65},{2,34}... | collective-permute-start | bytes 393224 | tf_op jit(solution)/shard_map/ppermute | solution.py:230
  76.3 14.3 %collective-permute-start.1 = (f32[128,256]{1,0:T(8,128)}, f32[128,256]{1,0:T(8,128)S(1)}, u32[]{:S(2)}, u32[]{:S(2)}) collective-permute-start(f32[128,256]{1,0:T(8,128)} %get-tuple-element.13), channel_id=1, source_target_pairs={{0,96},{32,64},{64,32},{96,0},{1,97},{33,65},{65,33},{97,1},{2,98}... | collective-permute-start | bytes 393224 | tf_op jit(solution)/shard_map/ppermute | solution.py:230
Sparse Core Ops, SparseCore 0:
  108.1 16.2 all-gather.4

commit v2 on v1

--- a/solution.py
+++ b/solution.py
@@ -13,6 +13,7 @@
 H = 128
 PACK = 272
 NS_STEPS = 3
+VMEM_BYTES = 8 * 1024 * 1024
 
 
 def split(a):
@@ -138,7 +139,7 @@
             out_ref[...] = mm(split(out_ref[...]), split(t))
 
 
-def pair_kernel(first_of, copies, mine_ref, other_ref, total_ref, half_ref):
+def pair_kernel(first_of, mine_ref, other_ref, total_ref, half_ref):
     first = first_of(lax.axis_index("zh"))
 
     @pl.when(first)
@@ -150,12 +151,7 @@
         total_ref[...] = mm(split(other_ref[...]), split(mine_ref[...]))
 
     core = lax.axis_index("core")
-    half = total_ref[pl.ds(pl.multiple_of(core * H, 8), H), :]
-    if copies:
-        for copy in range(copies):
-            half_ref[copy] = half
-    else:
-        half_ref[...] = half
+    half_ref[...] = total_ref[pl.ds(pl.multiple_of(core * H, 8), H), :]
 
 
 def pair_apply_kernel(first_of, other_ref, cur_ref, out_ref):
@@ -170,15 +166,22 @@
         out_ref[...] = cur_ref[...]
 
 
-def row_apply_kernel(parts_ref, cur_ref, out_ref):
+def row_apply_kernel(whole_ref, half_ref, cur_ref, out_ref):
     mine = lax.axis_index("y")
     out_ref[...] = cur_ref[...]
-    for place in range(1, 4):
-
-        @pl.when(place > mine)
-        def _():
-            t = jnp.concatenate([parts_ref[0, place], parts_ref[1, place]], axis=0)
-            out_ref[...] = mm(split(out_ref[...]), split(t))
+
+    @pl.when(mine < 3)
+    def _():
+        out_ref[...] = mm(split(out_ref[...]), split(whole_ref[0]))
+
+    @pl.when(mine < 2)
+    def _():
+        second = jnp.concatenate([half_ref[0], half_ref[1]], axis=0)
+        out_ref[...] = mm(split(out_ref[...]), split(second))
+
+    @pl.when(mine < 1)
+    def _():
+        out_ref[...] = mm(split(out_ref[...]), split(whole_ref[1]))
 
 
 VMEM = pl.BlockSpec(memory_space=pltpu.VMEM)
@@ -195,6 +198,7 @@
         in_specs=[VMEM] * len(args),
         out_specs=[VMEM] * len(shapes) if many else VMEM,
         scratch_shapes=list(scratch),
+        compiler_params=pltpu.CompilerParams(vmem_limit_bytes=VMEM_BYTES),
         cost_estimate=pl.CostEstimate(
             flops=products * 6 * N * N * N, bytes_accessed=moved, transcendentals=0
         ),
@@ -211,6 +215,18 @@
 
 PAIR_ONE = [(quad, quad ^ 1) for quad in range(4)]
 PAIR_TWO = [(quad, quad ^ 3) for quad in range(4)]
+
+
+def from_later(steps):
+    return [
+        (2 * row + core, 2 * (row - back) + core)
+        for core, back in enumerate(steps)
+        for row in range(back, 4)
+    ]
+
+
+ROW_ODD = from_later((1, 3))
+ROW_EVEN = from_later((2, 2))
 
 
 def shards(anomalies, mean_state, obs_rows, obs_precision):
@@ -226,22 +242,18 @@
     full = (N, N)
     total, half = call(quad_kernel, "quad", [full, (H, N)], (parts,), 3)
     current = call(quad_apply_kernel, "quad_apply", full, (parts, current), 4)
-    for pairs, first_of, copies in ((PAIR_ONE, in_left_quad, 0), (PAIR_TWO, in_left_half, 4)):
+    for pairs, first_of in ((PAIR_ONE, in_left_quad), (PAIR_TWO, in_left_half)):
         other = lax.ppermute(half, "zh", pairs)
         other = lax.all_gather(other, "core", tiled=True)
-        half_shape = (copies, H, N) if copies else (H, N)
         total, half = call(
-            functools.partial(pair_kernel, first_of, copies),
-            "pair",
-            [full, half_shape],
-            (total, other),
-            1,
+            functools.partial(pair_kernel, first_of), "pair", [full, (H, N)], (total, other), 1
         )
         current = call(
             functools.partial(pair_apply_kernel, first_of), "pair_apply", full, (other, current), 1
         )
-    parts = lax.all_gather(lax.all_to_all(half, "y", 0, 0), "core")
-    return call(row_apply_kernel, "row_apply", full, (parts, current), 3)[None]
+    whole = lax.all_gather(lax.ppermute(total, ("y", "core"), ROW_ODD), "core")
+    half = lax.all_gather(lax.ppermute(half, ("y", "core"), ROW_EVEN), "core")
+    return call(row_apply_kernel, "row_apply", full, (whole, half, current), 3)[None]
 
 
 def solution(mesh):

time: 135 us -> 97.4 us (0.72)
  Pallas kernels: 23.2 us -> 7.82 us
  between operations: 13.4 us -> 0.12 us
  blocking collectives: 54.1 us -> 44 us
  waiting for transfers between devices: 32 us -> 26.1 us
  starting transfers between devices: 11.3 us -> 15.8 us
  local copies, waits for them, and re-layouts: 0.04 us -> 2.34 us
    pallas_call x9, Pallas kernels: 23.2 us -> 7.82 us  [call(): pl.pallas_call(kernel, name=name, out_shape=shapes if many else shapes[0]...]
    all_to_all x1 -> x0, blocking collectives: 12.9 us -> none  [shards(): parts = lax.all_gather(lax.all_to_all(half, 'y', 0, 0), 'core')]
    all_gather x1 -> x0, waiting for transfers between devices: 9.16 us -> none  [shards(): parts = lax.all_gather(lax.all_to_all(half, 'y', 0, 0), 'core')]
    all_gather x0 -> x2, blocking collectives: none -> 5.18 us  [the longest x1 3.01 us: shards(): half = lax.all_gather(lax.ppermute(half, ('y', 'core'), ROW_EVEN), 'core')]
    ppermute x0 -> x2, waiting for transfers between devices: none -> 4.63 us  [the longest x1 4.63 us: shards(): half = lax.all_gather(lax.ppermute(half, ('y', 'core'), ROW_EVEN), 'core')]
    ppermute x0 -> x2, starting transfers between devices: none -> 2.58 us  [the longest x1 1.29 us: shards(): whole = lax.all_gather(lax.ppermute(total, ('y', 'core'), ROW_ODD), 'core')]
    unnamed x0 -> x10, local copies, waits for them, and re-layouts: none -> 2.3 us
    ppermute x2, starting transfers between devices: 11.3 us -> 13.2 us  [shards(): other = lax.ppermute(half, 'zh', pairs)]
  transfers between devices with their start and end apart: 3 -> 4, of which waited for: 3 -> 3; matrix products, arithmetic and copies ran while one was open for 0% -> 0% of each run, Pallas kernels for 5% -> 2%
where the time goes in v2:
time: 97.4 us; the launch traced here: 96.1 us
  blocking collectives  44 us (45%)
  waiting for transfers between devices  26.1 us (27%)
  starting transfers between devices  15.8 us (16%)
  Pallas kernels  7.82 us (8%)
  local copies, waits for them, and re-layouts  2.34 us (2%)
    ppermute x2, waiting for transfers between devices, shards(): other = lax.ppermute(half, 'zh', pairs)  21.4 us
    ppermute x2, starting transfers between devices, shards(): other = lax.ppermute(half, 'zh', pairs)  13.2 us
    all_to_all x1, blocking collectives, shards(): parts = lax.all_to_all(spread, 'x', 0, 0)  11.8 us
    all_to_all x1, blocking collectives, shards(): parts = lax.all_gather(lax.all_to_all(half, 'zl', 0, 0), 'core')  9.56 us
    all_gather x1, blocking collectives, shards(): both = lax.all_gather(gram, 'core')  8.48 us
    pallas_call x9, Pallas kernels, call(): pl.pallas_call(kernel, name=name, out_shape=shapes if many else shapes[0]...  7.82 us
    all_gather x1, blocking collectives, shards(): parts = lax.all_gather(lax.all_to_all(half, 'zl', 0, 0), 'core')  4.8 us
    ppermute x1, waiting for transfers between devices, shards(): half = lax.all_gather(lax.ppermute(half, ('y', 'core'), ROW_EVEN), 'core')  4.63 us
  transfers between devices with their start and end apart: 4, of which 3 were waited for; matrix products, arithmetic and copies ran while one was open for 0% of the time, Pallas kernels for 2%

profile of v2, /device:TPU:1, one launch (start us, length us, event | category | flops | bytes accessed | tf_op | source)
XLA Modules:
  0.0 96.1 jit_solution(12978804766842424211)
XLA Ops:
  0.0 0.0 copy-start.3
  0.0 0.0 copy-start.2
  0.0 0.7 copy-done.3
  0.7 0.0 copy-done.2
  0.7 0.0 copy-start
  0.7 0.9 copy-done
  1.6 0.0 copy-start.4
  1.6 0.7 copy-done.4
  2.3 0.8 gram.1
  3.1 8.5 %all-gather = f32[544,128]{1,0:T(8,128)S(1)} all-gather(f32[272,128]{1,0:T(8,128)S(1)} %gram.1), channel_id=2, replica_groups=mesh['y'=4,'zh'=4,'zl'=4,'x'=4,'core'=2] {'core'}, dimensions={0}, use_global_device_ids=true | all-gather | bytes 417792 | tf_op jit(solution)/shard_map/all_gather | solution.py:235
  11.6 11.8 %all_to_all.10.parts_ref = f32[4,272,128]{2,1,0:T(8,128)S(1)} all-to-all(f32[4,272,128]{2,1,0:T(8,128)S(1)} %broadcast_in_dim.6), channel_id=1, replica_groups=mesh['y'=4,'zh'=4,'zl'=4,'x'=4,'core'=2] {'x'}, dimensions={0} | all-to-all | bytes 1114112 | tf_op jit(solution)/shard_map/all_to_all | solution.py:237
  23.5 1.9 %root.1 = f32[4,136,128]{2,1,0:T(8,128)S(1)} custom-call(f32[4,272,128]{2,1,0:T(8,128)S(1)} %all_to_all.10.parts_ref), custom_call_target="tpu_custom_call" | custom-call | flops 603979776 | bytes 835584 | tf_op jit(solution)/shard_map/root/pallas_call | solution.py:194
  25.4 9.6 %all_to_all.11 = f32[4,136,128]{2,1,0:T(8,128)S(1)} all-to-all(f32[4,136,128]{2,1,0:T(8,128)S(1)} %root.1), channel_id=1, replica_groups=mesh['y'=4,'zh'=4,'zl'=4,'x'=4,'core'=2] {'zl'}, dimensions={0} | all-to-all | bytes 557056 | tf_op jit(solution)/shard_map/all_to_all | solution.py:241
  35.0 4.8 %all-gather.1 = f32[8,136,128]{2,1,0:T(8,128)S(1)} all-gather(f32[4,136,128]{2,1,0:T(8,128)S(1)} %all_to_all.11), channel_id=3, replica_groups=mesh['y'=4,'zh'=4,'zl'=4,'x'=4,'core'=2] {'core'}, dimensions={0}, use_global_device_ids=true | all-gather | bytes 835584 | tf_op jit(solution)/shard_map/all_gather | solution.py:241
  39.8 0.9 quad.1
  40.7 7.8 %collective-permute-start = (f32[128,256]{1,0:T(8,128)S(1)}, f32[128,256]{1,0:T(8,128)S(1)}, u32[]{:S(2)}, u32[]{:S(2)}) collective-permute-start(f32[128,256]{1,0:T(8,128)S(1)} %get-tuple-element.12), channel_id=1, source_target_pairs={{0,32},{32,0},{64,96},{96,64},{1,33},{33,1},{65,97},{97,65},{2,34}... | collective-permute-start | bytes 393224 | tf_op jit(solution)/shard_map/ppermute | solution.py:246
  48.5 12.4 %collective-permute-done = f32[128,256]{1,0:T(8,128)S(1)} collective-permute-done((f32[128,256]{1,0:T(8,128)S(1)}, f32[128,256]{1,0:T(8,128)S(1)}, u32[]{:S(2)}, u32[]{:S(2)}) %collective-permute-start) | collective-permute-done | bytes 131104 | tf_op jit(solution)/shard_map/ppermute | solution.py:246
  60.9 2.1 %all_gather.34.other_ref = f32[256,256]{1,0:T(8,128)S(1)} all-gather(f32[128,256]{1,0:T(8,128)S(1)} %collective-permute-done), channel_id=1, replica_groups=mesh['y'=4,'zh'=4,'zl'=4,'x'=4,'core'=2] {'core'}, dimensions={0}, use_global_device_ids=true | all-gather | bytes 393216 | tf_op jit(solution)/shard_map/all_gather | solution.py:247
  62.9 0.3 pair.2
  63.2 5.4 %collective-permute-start.1 = (f32[128,256]{1,0:T(8,128)S(1)}, f32[128,256]{1,0:T(8,128)S(1)}, u32[]{:S(2)}, u32[]{:S(2)}) collective-permute-start(f32[128,256]{1,0:T(8,128)S(1)} %get-tuple-element.14), channel_id=1, source_target_pairs={{0,96},{32,64},{64,32},{96,0},{1,97},{33,65},{65,33},{97,1},{2,98}... | collective-permute-start | bytes 393224 | tf_op jit(solution)/shard_map/ppermute | solution.py:246
  68.6 9.1 %collective-permute-done.1 = f32[128,256]{1,0:T(8,128)S(1)} collective-permute-done((f32[128,256]{1,0:T(8,128)S(1)}, f32[128,256]{1,0:T(8,128)S(1)}, u32[]{:S(2)}, u32[]{:S(2)}) %collective-permute-start.1) | collective-permute-done | bytes 131104 | tf_op jit(solution)/shard_map/ppermute | solution.py:246
  77.7 2.1 %all_gather.35.other_ref = f32[256,256]{1,0:T(8,128)S(1)} all-gather(f32[128,256]{1,0:T(8,128)S(1)} %collective-permute-done.1), channel_id=1, replica_groups=mesh['y'=4,'zh'=4,'zl'=4,'x'=4,'core'=2] {'core'}, dimensions={0}, use_global_device_ids=true | all-gather | bytes 393216 | tf_op jit(solution)/shard_map/all_gather | solution.py:247
  79.8 0.0 copy-start.1
  79.8 0.3 pair.3
  80.1 1.3 %collective-permute-start.2 = (f32[256,256]{1,0:T(8,128)S(1)}, f32[256,256]{1,0:T(8,128)S(1)}, u32[]{:S(2)}, u32[]{:S(2)}) collective-permute-start(f32[256,256]{1,0:T(8,128)S(1)} %get-tuple-element.15), channel_id=1, source_target_pairs={{128,0},{256,128},{384,256},{385,1},{130,2},{258,130},{386,258},{3... | collective-permute-start | bytes 786440 | tf_op jit(solution)/shard_map/ppermute | solution.py:254
  81.4 1.3 %collective-permute-start.3 = (f32[128,256]{1,0:T(8,128)S(1)}, f32[128,256]{1,0:T(8,128)S(1)}, u32[]{:S(2)}, u32[]{:S(2)}) collective-permute-start(f32[128,256]{1,0:T(8,128)S(1)} %get-tuple-element.16), channel_id=1, source_target_pairs={{256,0},{384,128},{257,1},{385,129},{258,2},{386,130},{259,3},{387... | collective-permute-start | bytes 393224 | tf_op jit(solution)/shard_map/ppermute | solution.py:255
  82.7 0.0 copy-done.1
  82.7 1.5 %quad_apply.1.cur_ref = f32[256,256]{1,0:T(8,128)S(1)} custom-call(f32[2,4,136,128]{3,2,1,0:T(8,128)S(1)} %bitcast.8, f32[256,256]{1,0:T(8,128)S(1)} %bitcast.10), custom_call_target="tpu_custom_call" | custom-call | flops 402653184 | bytes 1081344 | tf_op jit(solution)/shard_map/quad_apply/pallas_call | solution.py:194
  84.2 0.3 pair_apply.2.cur_ref
  84.5 0.3 pair_apply.3.cur_ref
  84.8 4.6 %collective-permute-done.3 = f32[128,256]{1,0:T(8,128)S(1)} collective-permute-done((f32[128,256]{1,0:T(8,128)S(1)}, f32[128,256]{1,0:T(8,128)S(1)}, u32[]{:S(2)}, u32[]{:S(2)}) %collective-permute-start.3) | collective-permute-done | bytes 131104 | tf_op jit(solution)/shard_map/ppermute | solution.py:255
  89.4 3.0 %all-gather.3 = f32[256,256]{1,0:T(8,128)S(1)} all-gather(f32[128,256]{1,0:T(8,128)S(1)} %collective-permute-done.3), channel_id=5, replica_groups=mesh['y'=4,'zh'=4,'zl'=4,'x'=4,'core'=2] {'core'}, dimensions={0}, use_global_device_ids=true | all-gather | bytes 393216 | tf_op jit(solution)/shard_map/all_gather | solution.py:255
  92.4 0.0 collective-permute-done.2
  92.4 2.2 %all-gather.2 = f32[512,256]{1,0:T(8,128)S(1)} all-gather(f32[256,256]{1,0:T(8,128)S(1)} %collective-permute-done.2), channel_id=4, replica_groups=mesh['y'=4,'zh'=4,'zl'=4,'x'=4,'core'=2] {'core'}, dimensions={0}, use_global_device_ids=true | all-gather | bytes 786432 | tf_op jit(solution)/shard_map/all_gather | solution.py:254
  94.6 1.6 %row_apply.1 = f32[256,256]{1,0:T(8,128)} custom-call(f32[2,256,256]{2,1,0:T(8,128)S(1)} %bitcast.5, f32[2,128,256]{2,1,0:T(8,128)S(1)} %bitcast.6, f32[256,256]{1,0:T(8,128)S(1)} %pair_apply.3.cur_ref), custom_call_target="tpu_custom_call" | custom-call | flops 301989888 | bytes 1310720 | tf_op jit(solution)/shard_map/row_apply/pallas_call | solution.py:194
  (2 shorter events, 0.1 us)
Async XLA Ops:
  0.0 0.7 copy-start.3
  0.0 0.7 copy-start.2
  0.7 0.9 copy-start
  1.6 0.7 copy-start.4
  40.7 20.2 %collective-permute-start = (f32[128,256]{1,0:T(8,128)S(1)}, f32[128,256]{1,0:T(8,128)S(1)}, u32[]{:S(2)}, u32[]{:S(2)}) collective-permute-start(f32[128,256]{1,0:T(8,128)S(1)} %get-tuple-element.12), channel_id=1, source_target_pairs={{0,32},{32,0},{64,96},{96,64},{1,33},{33,1},{65,97},{97,65},{2,34}... | collective-permute-start | bytes 393224 | tf_op jit(solution)/shard_map/ppermute | solution.py:246
  63.2 14.4 %collective-permute-start.1 = (f32[128,256]{1,0:T(8,128)S(1)}, f32[128,256]{1,0:T(8,128)S(1)}, u32[]{:S(2)}, u32[]{:S(2)}) collective-permute-start(f32[128,256]{1,0:T(8,128)S(1)} %get-tuple-element.14), channel_id=1, source_target_pairs={{0,96},{32,64},{64,32},{96,0},{1,97},{33,65},{65,33},{97,1},{2,98}... | collective-permute-start | bytes 393224 | tf_op jit(solution)/shard_map/ppermute | solution.py:246
  79.8 2.9 %copy-start.1 = (f32[1,256,256]{2,1,0:T(8,128)S(1)}, f32[1,256,256]{2,1,0:T(8,128)}, u32[]{:S(2)}) copy-start(f32[1,256,256]{2,1,0:T(8,128)} %param.4) | copy-start | bytes 786436
  80.1 12.3 %collective-permute-start.2 = (f32[256,256]{1,0:T(8,128)S(1)}, f32[256,256]{1,0:T(8,128)S(1)}, u32[]{:S(2)}, u32[]{:S(2)}) collective-permute-start(f32[256,256]{1,0:T(8,128)S(1)} %get-tuple-element.15), channel_id=1, source_target_pairs={{128,0},{256,128},{384,256},{385,1},{130,2},{258,130},{386,258},{3... | collective-permute-start | bytes 786440 | tf_op jit(solution)/shard_map/ppermute | solution.py:254
  81.4 8.0 %collective-permute-start.3 = (f32[128,256]{1,0:T(8,128)S(1)}, f32[128,256]{1,0:T(8,128)S(1)}, u32[]{:S(2)}, u32[]{:S(2)}) collective-permute-start(f32[128,256]{1,0:T(8,128)S(1)} %get-tuple-element.16), channel_id=1, source_target_pairs={{256,0},{384,128},{257,1},{385,129},{258,2},{386,130},{259,3},{387... | collective-permute-start | bytes 393224 | tf_op jit(solution)/shard_map/ppermute | solution.py:255

commit v3 on v2

--- a/solution.py
+++ b/solution.py
@@ -13,6 +13,7 @@
 H = 128
 PACK = 272
 NS_STEPS = 3
+ALL_VMEM = 67043328
 VMEM_BYTES = 8 * 1024 * 1024
 
 
@@ -60,7 +61,17 @@
     return jnp.concatenate([top, low], axis=0)
 
 
-def gram_kernel(cur_ref, mean_ref, rows_ref, prec_ref, out_ref):
+def gram_kernel(*refs):
+    sources, out_ref, held, sems = refs[:4], refs[4], refs[5:9], refs[9]
+    copies = [
+        pltpu.make_async_copy(source, target, sems.at[place])
+        for place, (source, target) in enumerate(zip(sources, held))
+    ]
+    for copy in copies:
+        copy.start()
+    for copy in copies:
+        copy.wait()
+    cur_ref, mean_ref, rows_ref, prec_ref = held
     value = cur_ref[...] + column(mean_ref[...], N)
     state_row = lax.broadcasted_iota(jnp.int32, (N, H), 0)
     chosen = (state_row == rows_ref[...]).astype(F32).T.astype(BF16)
@@ -139,55 +150,57 @@
             out_ref[...] = mm(split(out_ref[...]), split(t))
 
 
-def pair_kernel(first_of, mine_ref, other_ref, total_ref, half_ref):
-    first = first_of(lax.axis_index("zh"))
-
-    @pl.when(first)
-    def _():
-        total_ref[...] = mm(split(mine_ref[...]), split(other_ref[...]))
-
-    @pl.when(jnp.logical_not(first))
-    def _():
-        total_ref[...] = mm(split(other_ref[...]), split(mine_ref[...]))
+def ring_kernel(near_ref, mine_ref, total_ref, half_ref, one, two):
+    quad = lax.axis_index("zh")
+    mine = split(mine_ref[...])
+    after = split(near_ref[0, :N])
+    before = split(near_ref[1, :N])
+    across = split(jnp.concatenate([near_ref[0, N:], near_ref[1, N:]], axis=0))
+
+    @pl.when(quad % 2 == 0)
+    def _():
+        one[...] = mm(mine, after)
+        two[...] = mm(across, before)
+
+    @pl.when(quad % 2 == 1)
+    def _():
+        one[...] = mm(before, mine)
+        two[...] = mm(after, across)
+
+    @pl.when(quad < 2)
+    def _():
+        total_ref[...] = mm(split(one[...]), split(two[...]))
+
+    @pl.when(quad >= 2)
+    def _():
+        total_ref[...] = mm(split(two[...]), split(one[...]))
 
     core = lax.axis_index("core")
     half_ref[...] = total_ref[pl.ds(pl.multiple_of(core * H, 8), H), :]
 
 
-def pair_apply_kernel(first_of, other_ref, cur_ref, out_ref):
-    first = first_of(lax.axis_index("zh"))
-
-    @pl.when(first)
-    def _():
-        out_ref[...] = mm(split(cur_ref[...]), split(other_ref[...]))
-
-    @pl.when(jnp.logical_not(first))
-    def _():
-        out_ref[...] = cur_ref[...]
-
-
-def row_apply_kernel(whole_ref, half_ref, cur_ref, out_ref):
-    mine = lax.axis_index("y")
+def apply_kernel(axis, near_ref, cur_ref, out_ref):
+    mine = lax.axis_index(axis)
     out_ref[...] = cur_ref[...]
 
     @pl.when(mine < 3)
     def _():
-        out_ref[...] = mm(split(out_ref[...]), split(whole_ref[0]))
+        out_ref[...] = mm(split(out_ref[...]), split(near_ref[0, :N]))
 
     @pl.when(mine < 2)
     def _():
-        second = jnp.concatenate([half_ref[0], half_ref[1]], axis=0)
+        second = jnp.concatenate([near_ref[0, N:], near_ref[1, N:]], axis=0)
         out_ref[...] = mm(split(out_ref[...]), split(second))
 
     @pl.when(mine < 1)
     def _():
-        out_ref[...] = mm(split(out_ref[...]), split(whole_ref[1]))
+        out_ref[...] = mm(split(out_ref[...]), split(near_ref[1, :N]))
 
 
 VMEM = pl.BlockSpec(memory_space=pltpu.VMEM)
 
 
-def call(kernel, name, outs, args, products, scratch=()):
+def call(kernel, name, outs, args, products, scratch=(), space=VMEM, limit=VMEM_BYTES):
     many = isinstance(outs, list)
     shapes = [jax.ShapeDtypeStruct(s, F32) for s in (outs if many else [outs])]
     moved = sum(a.size * 4 for a in args) + sum(s.size * 4 for s in shapes)
@@ -195,26 +208,23 @@
         kernel,
         name=name,
         out_shape=shapes if many else shapes[0],
-        in_specs=[VMEM] * len(args),
+        in_specs=[space] * len(args),
         out_specs=[VMEM] * len(shapes) if many else VMEM,
         scratch_shapes=list(scratch),
-        compiler_params=pltpu.CompilerParams(vmem_limit_bytes=VMEM_BYTES),
+        compiler_params=pltpu.CompilerParams(vmem_limit_bytes=limit),
         cost_estimate=pl.CostEstimate(
             flops=products * 6 * N * N * N, bytes_accessed=moved, transcendentals=0
         ),
     )(*args)
 
 
-def in_left_quad(quad):
-    return quad % 2 == 0
-
-
-def in_left_half(quad):
-    return quad < 2
-
-
-PAIR_ONE = [(quad, quad ^ 1) for quad in range(4)]
-PAIR_TWO = [(quad, quad ^ 3) for quad in range(4)]
+RING = 16
+NEAR = [
+    (2 * z + core, 2 * ((z + step) % RING) + core)
+    for core, step in enumerate((-4, 4))
+    for z in range(RING)
+]
+ACROSS = [(z, (11 - z) if z % 8 < 4 else (19 - z)) for z in range(RING)]
 
 
 def from_later(steps):
@@ -231,7 +241,17 @@
 
 def shards(anomalies, mean_state, obs_rows, obs_precision):
     current = anomalies[0]
-    gram = call(gram_kernel, "gram", (PACK, H), (current, mean_state, obs_rows, obs_precision), 1)
+    sources = (current, mean_state, obs_rows, obs_precision)
+    gram = call(
+        gram_kernel,
+        "gram",
+        (PACK, H),
+        sources,
+        1,
+        [pltpu.VMEM(a.shape, a.dtype) for a in sources] + [pltpu.SemaphoreType.DMA((4,))],
+        pl.BlockSpec(memory_space=pltpu.HBM),
+        ALL_VMEM - PACK * H * 4,
+    )
     both = lax.all_gather(gram, "core")
     spread = jnp.broadcast_to(both[0] + both[1], (4, PACK, H))
     parts = lax.all_to_all(spread, "x", 0, 0)
@@ -242,18 +262,20 @@
     full = (N, N)
     total, half = call(quad_kernel, "quad", [full, (H, N)], (parts,), 3)
     current = call(quad_apply_kernel, "quad_apply", full, (parts, current), 4)
-    for pairs, first_of in ((PAIR_ONE, in_left_quad), (PAIR_TWO, in_left_half)):
-        other = lax.ppermute(half, "zh", pairs)
-        other = lax.all_gather(other, "core", tiled=True)
-        total, half = call(
-            functools.partial(pair_kernel, first_of), "pair", [full, (H, N)], (total, other), 1
-        )
-        current = call(
-            functools.partial(pair_apply_kernel, first_of), "pair_apply", full, (other, current), 1
-        )
-    whole = lax.all_gather(lax.ppermute(total, ("y", "core"), ROW_ODD), "core")
-    half = lax.all_gather(lax.ppermute(half, ("y", "core"), ROW_EVEN), "core")
-    return call(row_apply_kernel, "row_apply", full, (whole, half, current), 3)[None]
+    across = lax.ppermute(half, ("zh", "zl"), ACROSS)
+    near = lax.ppermute(total, ("zh", "zl", "core"), NEAR)
+    near = lax.all_gather(jnp.concatenate([near, across], axis=0), "core")
+    square = pltpu.VMEM(full, F32)
+    total, half = call(
+        ring_kernel, "ring", [full, (H, N)], (near, total), 3, [square, square]
+    )
+    current = call(
+        functools.partial(apply_kernel, "zh"), "ring_apply", full, (near, current), 3
+    )
+    near = lax.ppermute(total, ("y", "core"), ROW_ODD)
+    half = lax.ppermute(half, ("y", "core"), ROW_EVEN)
+    near = lax.all_gather(jnp.concatenate([near, half], axis=0), "core")
+    return call(functools.partial(apply_kernel, "y"), "row_apply", full, (near, current), 3)[None]
 
 
 def solution(mesh):

time: 97.4 us -> 92.9 us (0.954)
  blocking collectives: 44 us -> 39.6 us
  local copies, waits for them, and re-layouts: 2.34 us -> 0.04 us
  Pallas kernels: 7.82 us -> 10 us
    all_gather x4 -> x2, blocking collectives: 9.34 us -> 4.74 us  [the longest x1 2.37 us: shards(): near = lax.all_gather(jnp.concatenate([near, across], axis=0), 'core')]
    unnamed x10 -> x2, local copies, waits for them, and re-layouts: 2.3 us -> 0.01 us
    pallas_call x9 -> x7, Pallas kernels: 7.82 us -> 10 us  [call(): pl.pallas_call(kernel, name=name, out_shape=shapes if many else shapes[0]...]
  transfers between devices with their start and end apart: 4 -> 4, of which waited for: 3 -> 3; matrix products, arithmetic and copies ran while one was open for 0% -> 0% of each run, Pallas kernels for 2% -> 3%
where the time goes in v3:
time: 92.9 us; the launch traced here: 92.6 us
  blocking collectives  39.6 us (43%)
  waiting for transfers between devices  26.2 us (28%)
  starting transfers between devices  16.5 us (18%)
  Pallas kernels  10 us (11%)
    ppermute x1, waiting for transfers between devices, shards(): across = lax.ppermute(half, ('zh', 'zl'), ACROSS)  20 us
    all_to_all x1, blocking collectives, shards(): parts = lax.all_to_all(spread, 'x', 0, 0)  11.8 us
    pallas_call x7, Pallas kernels, call(): pl.pallas_call(kernel, name=name, out_shape=shapes if many else shapes[0]...  10 us
    all_to_all x1, blocking collectives, shards(): parts = lax.all_gather(lax.all_to_all(half, 'zl', 0, 0), 'core')  9.56 us
    all_gather x1, blocking collectives, shards(): both = lax.all_gather(gram, 'core')  8.69 us
    ppermute x1, starting transfers between devices, shards(): near = lax.ppermute(total, ('zh', 'zl', 'core'), NEAR)  7.8 us
    ppermute x1, starting transfers between devices, shards(): across = lax.ppermute(half, ('zh', 'zl'), ACROSS)  6.14 us
    all_gather x1, blocking collectives, shards(): parts = lax.all_gather(lax.all_to_all(half, 'zl', 0, 0), 'core')  4.8 us
  transfers between devices with their start and end apart: 4, of which 3 were waited for; matrix products, arithmetic and copies ran while one was open for 0% of the time, Pallas kernels for 3%

profile of v3, /device:TPU:1, one launch (start us, length us, event | category | flops | bytes accessed | tf_op | source)
XLA Modules:
  0.0 92.6 jit_solution(7822329006671662610)
XLA Ops:
  0.0 2.4 %gram.1 = f32[272,128]{1,0:T(8,128)} custom-call(f32[256,256]{1,0:T(8,128)} %bitcast.10, f32[1,256]{1,0:T(1,128)} %refs_1_.1, s32[1,128]{1,0:T(1,128)} %refs_2_.1, f32[1,128]{1,0:T(1,128)} %refs_3_.1), custom_call_target="tpu_custom_call" | custom-call | flops 100663296 | bytes 403456 | tf_op jit(solution)/shard_map/gram/pallas_call | solution.py:207
  2.5 8.7 %all-gather = f32[544,128]{1,0:T(8,128)S(1)} all-gather(f32[272,128]{1,0:T(8,128)} %gram.1), channel_id=2, replica_groups=mesh['y'=4,'zh'=4,'zl'=4,'x'=4,'core'=2] {'core'}, dimensions={0}, use_global_device_ids=true | all-gather | bytes 417792 | tf_op jit(solution)/shard_map/all_gather | solution.py:255
  11.2 11.8 %all_to_all.10.parts_ref = f32[4,272,128]{2,1,0:T(8,128)S(1)} all-to-all(f32[4,272,128]{2,1,0:T(8,128)S(1)} %broadcast_in_dim.6), channel_id=1, replica_groups=mesh['y'=4,'zh'=4,'zl'=4,'x'=4,'core'=2] {'x'}, dimensions={0} | all-to-all | bytes 1114112 | tf_op jit(solution)/shard_map/all_to_all | solution.py:257
  23.0 1.9 %root.1 = f32[4,136,128]{2,1,0:T(8,128)S(1)} custom-call(f32[4,272,128]{2,1,0:T(8,128)S(1)} %all_to_all.10.parts_ref), custom_call_target="tpu_custom_call" | custom-call | flops 603979776 | bytes 835584 | tf_op jit(solution)/shard_map/root/pallas_call | solution.py:207
  25.0 9.6 %all_to_all.11 = f32[4,136,128]{2,1,0:T(8,128)S(1)} all-to-all(f32[4,136,128]{2,1,0:T(8,128)S(1)} %root.1), channel_id=1, replica_groups=mesh['y'=4,'zh'=4,'zl'=4,'x'=4,'core'=2] {'zl'}, dimensions={0} | all-to-all | bytes 557056 | tf_op jit(solution)/shard_map/all_to_all | solution.py:261
  34.5 4.8 %all-gather.1 = f32[8,136,128]{2,1,0:T(8,128)S(1)} all-gather(f32[4,136,128]{2,1,0:T(8,128)S(1)} %all_to_all.11), channel_id=3, replica_groups=mesh['y'=4,'zh'=4,'zl'=4,'x'=4,'core'=2] {'core'}, dimensions={0}, use_global_device_ids=true | all-gather | bytes 835584 | tf_op jit(solution)/shard_map/all_gather | solution.py:261
  39.3 0.9 quad.1
  40.3 7.8 %collective-permute-start = (f32[256,256]{1,0:T(8,128)S(1)}, f32[256,256]{1,0:T(8,128)S(1)}, u32[]{:S(2)}, u32[]{:S(2)}) collective-permute-start(f32[256,256]{1,0:T(8,128)S(1)} %get-tuple-element.9.mine_ref), channel_id=1, source_target_pairs={{0,96},{8,104},{16,112},{24,120},{32,0},{40,8},{48,16},{56,24},{64... | collective-permute-start | bytes 786440 | tf_op jit(solution)/shard_map/ppermute | solution.py:266
  48.1 6.1 %collective-permute-start.1 = (f32[128,256]{1,0:T(8,128)S(1)}, f32[128,256]{1,0:T(8,128)S(1)}, u32[]{:S(2)}, u32[]{:S(2)}) collective-permute-start(f32[128,256]{1,0:T(8,128)S(1)} %get-tuple-element.10), channel_id=1, source_target_pairs={{0,88},{8,80},{16,72},{24,64},{32,120},{40,112},{48,104},{56,96},{... | collective-permute-start | bytes 393224 | tf_op jit(solution)/shard_map/ppermute | solution.py:265
  54.2 20.0 %collective-permute-done.1 = f32[128,256]{1,0:T(8,128)S(1)} collective-permute-done((f32[128,256]{1,0:T(8,128)S(1)}, f32[128,256]{1,0:T(8,128)S(1)}, u32[]{:S(2)}, u32[]{:S(2)}) %collective-permute-start.1) | collective-permute-done | bytes 131104 | tf_op jit(solution)/shard_map/ppermute | solution.py:265
  74.2 0.0 collective-permute-done
  74.3 2.4 %all-gather.2 = f32[768,256]{1,0:T(8,128)S(1)} all-gather(f32[384,256]{1,0:T(8,128)S(1)} %pad_maximum_fusion), channel_id=4, replica_groups=mesh['y'=4,'zh'=4,'zl'=4,'x'=4,'core'=2] {'core'}, dimensions={0}, use_global_device_ids=true | all-gather | bytes 1179648 | tf_op jit(solution)/shard_map/all_gather | solution.py:267
  76.6 0.0 copy-start
  76.6 0.8 ring.1
  77.5 1.3 %collective-permute-start.2 = (f32[256,256]{1,0:T(8,128)S(1)}, f32[256,256]{1,0:T(8,128)S(1)}, u32[]{:S(2)}, u32[]{:S(2)}) collective-permute-start(f32[256,256]{1,0:T(8,128)S(1)} %get-tuple-element.11), channel_id=1, source_target_pairs={{128,0},{256,128},{384,256},{385,1},{130,2},{258,130},{386,258},{3... | collective-permute-start | bytes 786440 | tf_op jit(solution)/shard_map/ppermute | solution.py:275
  78.8 1.3 %collective-permute-start.3 = (f32[128,256]{1,0:T(8,128)S(1)}, f32[128,256]{1,0:T(8,128)S(1)}, u32[]{:S(2)}, u32[]{:S(2)}) collective-permute-start(f32[128,256]{1,0:T(8,128)S(1)} %get-tuple-element.12), channel_id=1, source_target_pairs={{256,0},{384,128},{257,1},{385,129},{258,2},{386,130},{259,3},{387... | collective-permute-start | bytes 393224 | tf_op jit(solution)/shard_map/ppermute | solution.py:276
  80.1 0.0 copy-done
  80.1 1.5 %quad_apply.1.cur_ref = f32[256,256]{1,0:T(8,128)S(1)} custom-call(f32[2,4,136,128]{3,2,1,0:T(8,128)S(1)} %bitcast.9, f32[256,256]{1,0:T(8,128)S(1)} %bitcast.11), custom_call_target="tpu_custom_call" | custom-call | flops 402653184 | bytes 1081344 | tf_op jit(solution)/shard_map/quad_apply/pallas_call | solution.py:207
  81.6 0.9 ring_apply.1.cur_ref
  82.4 4.6 %collective-permute-done.3 = f32[128,256]{1,0:T(8,128)S(1)} collective-permute-done((f32[128,256]{1,0:T(8,128)S(1)}, f32[128,256]{1,0:T(8,128)S(1)}, u32[]{:S(2)}, u32[]{:S(2)}) %collective-permute-start.3) | collective-permute-done | bytes 131104 | tf_op jit(solution)/shard_map/ppermute | solution.py:276
  87.0 1.6 %collective-permute-done.2 = f32[256,256]{1,0:T(8,128)S(1)} collective-permute-done((f32[256,256]{1,0:T(8,128)S(1)}, f32[256,256]{1,0:T(8,128)S(1)}, u32[]{:S(2)}, u32[]{:S(2)}) %collective-permute-start.2) | collective-permute-done | bytes 262176 | tf_op jit(solution)/shard_map/ppermute | solution.py:275
  88.7 2.4 %all-gather.3 = f32[768,256]{1,0:T(8,128)S(1)} all-gather(f32[384,256]{1,0:T(8,128)S(1)} %pad_maximum_fusion.1), channel_id=5, replica_groups=mesh['y'=4,'zh'=4,'zl'=4,'x'=4,'core'=2] {'core'}, dimensions={0}, use_global_device_ids=true | all-gather | bytes 1179648 | tf_op jit(solution)/shard_map/all_gather | solution.py:277
  91.0 1.6 %row_apply.1 = f32[256,256]{1,0:T(8,128)} custom-call(f32[2,384,256]{2,1,0:T(8,128)S(1)} %bitcast.7, f32[256,256]{1,0:T(8,128)S(1)} %ring_apply.1.cur_ref), custom_call_target="tpu_custom_call" | custom-call | flops 301989888 | bytes 1310720 | tf_op jit(solution)/shard_map/row_apply/pallas_call | solution.py:207
  (4 shorter events, 0.1 us)
Async XLA Ops:
  40.3 34.0 %collective-permute-start = (f32[256,256]{1,0:T(8,128)S(1)}, f32[256,256]{1,0:T(8,128)S(1)}, u32[]{:S(2)}, u32[]{:S(2)}) collective-permute-start(f32[256,256]{1,0:T(8,128)S(1)} %get-tuple-element.9.mine_ref), channel_id=1, source_target_pairs={{0,96},{8,104},{16,112},{24,120},{32,0},{40,8},{48,16},{56,24},{64... | collective-permute-start | bytes 786440 | tf_op jit(solution)/shard_map/ppermute | solution.py:266
  48.1 26.2 %collective-permute-start.1 = (f32[128,256]{1,0:T(8,128)S(1)}, f32[128,256]{1,0:T(8,128)S(1)}, u32[]{:S(2)}, u32[]{:S(2)}) collective-permute-start(f32[128,256]{1,0:T(8,128)S(1)} %get-tuple-element.10), channel_id=1, source_target_pairs={{0,88},{8,80},{16,72},{24,64},{32,120},{40,112},{48,104},{56,96},{... | collective-permute-start | bytes 393224 | tf_op jit(solution)/shard_map/ppermute | solution.py:265
  76.6 3.4 %copy-start = (f32[1,256,256]{2,1,0:T(8,128)S(1)}, f32[1,256,256]{2,1,0:T(8,128)}, u32[]{:S(2)}) copy-start(f32[1,256,256]{2,1,0:T(8,128)} %param.4) | copy-start | bytes 786436
  77.5 11.1 %collective-permute-start.2 = (f32[256,256]{1,0:T(8,128)S(1)}, f32[256,256]{1,0:T(8,128)S(1)}, u32[]{:S(2)}, u32[]{:S(2)}) collective-permute-start(f32[256,256]{1,0:T(8,128)S(1)} %get-tuple-element.11), channel_id=1, source_target_pairs={{128,0},{256,128},{384,256},{385,1},{130,2},{258,130},{386,258},{3... | collective-permute-start | bytes 786440 | tf_op jit(solution)/shard_map/ppermute | solution.py:275
  78.8 8.2 %collective-permute-start.3 = (f32[128,256]{1,0:T(8,128)S(1)}, f32[128,256]{1,0:T(8,128)S(1)}, u32[]{:S(2)}, u32[]{:S(2)}) collective-permute-start(f32[128,256]{1,0:T(8,128)S(1)} %get-tuple-element.12), channel_id=1, source_target_pairs={{256,0},{384,128},{257,1},{385,129},{258,2},{386,130},{259,3},{387... | collective-permute-start | bytes 393224 | tf_op jit(solution)/shard_map/ppermute | solution.py:276

commit v4 on v3

--- a/solution.py
+++ b/solution.py
@@ -6,6 +6,7 @@
 from jax.experimental import pallas as pl
 from jax.experimental.pallas import tpu as pltpu
 from jax.sharding import Mesh, PartitionSpec as P
+
 
 F32 = jnp.float32
 BF16 = jnp.bfloat16
@@ -39,7 +40,7 @@
     return jnp.sum(jnp.where(i == j, row, 0.0), axis=1, keepdims=True)
 
 
-def pack(m, out, copies):
+def pack(m, out):
     i, j = eye_mask(H)
     first, corner = m[:H, :H], m[H:, H:]
     rows = jnp.where(i <= j, first, corner)
@@ -85,7 +86,7 @@
     centred = predicted - jnp.mean(predicted, axis=1, keepdims=True)
     centred = centred * jnp.sqrt(column(prec_ref[...], H))
     gram = mm(split(centred.T), split(centred)) * (1.0 / (N - 1))
-    pack(gram, out_ref, 1)
+    pack(gram, out_ref)
 
 
 def root_kernel(parts_ref, out_ref, packed):
@@ -106,7 +107,7 @@
         inverse = split(last)
     diag = jnp.where(i == j, last, 0.0)
     trace = jnp.sum(jnp.sum(diag, axis=0, keepdims=True), axis=1, keepdims=True)
-    pack(last * (N / trace), packed, 1)
+    pack(last * (N / trace), packed)
     core = lax.axis_index("core")
     half = packed[pl.ds(pl.multiple_of(core * (PACK // 2), 8), PACK // 2), :]
     for copy in range(4):
@@ -150,63 +151,82 @@
             out_ref[...] = mm(split(out_ref[...]), split(t))
 
 
-def ring_kernel(near_ref, mine_ref, total_ref, half_ref, one, two):
+def beside_kernel(near_ref, mine_ref, out_ref):
     quad = lax.axis_index("zh")
     mine = split(mine_ref[...])
-    after = split(near_ref[0, :N])
-    before = split(near_ref[1, :N])
-    across = split(jnp.concatenate([near_ref[0, N:], near_ref[1, N:]], axis=0))
 
     @pl.when(quad % 2 == 0)
     def _():
-        one[...] = mm(mine, after)
-        two[...] = mm(across, before)
+        out_ref[...] = mm(mine, split(near_ref[0]))
 
     @pl.when(quad % 2 == 1)
     def _():
-        one[...] = mm(before, mine)
-        two[...] = mm(after, across)
+        out_ref[...] = mm(split(near_ref[1]), mine)
+
+
+def ring_kernel(near_ref, across_ref, beside_ref, total_ref, half_ref, two):
+    quad = lax.axis_index("zh")
+    across = split(jnp.concatenate([across_ref[0], across_ref[1]], axis=0))
+    one = split(beside_ref[...])
+
+    @pl.when(quad % 2 == 0)
+    def _():
+        two[...] = mm(across, split(near_ref[1]))
+
+    @pl.when(quad % 2 == 1)
+    def _():
+        two[...] = mm(split(near_ref[0]), across)
 
     @pl.when(quad < 2)
     def _():
-        total_ref[...] = mm(split(one[...]), split(two[...]))
+        total_ref[...] = mm(one, split(two[...]))
 
     @pl.when(quad >= 2)
     def _():
-        total_ref[...] = mm(split(two[...]), split(one[...]))
+        total_ref[...] = mm(split(two[...]), one)
 
     core = lax.axis_index("core")
     half_ref[...] = total_ref[pl.ds(pl.multiple_of(core * H, 8), H), :]
 
 
-def apply_kernel(axis, near_ref, cur_ref, out_ref):
+def first_kernel(axis, near_ref, cur_ref, out_ref):
     mine = lax.axis_index(axis)
-    out_ref[...] = cur_ref[...]
 
     @pl.when(mine < 3)
     def _():
-        out_ref[...] = mm(split(out_ref[...]), split(near_ref[0, :N]))
+        out_ref[...] = mm(split(cur_ref[...]), split(near_ref[0]))
+
+    @pl.when(mine == 3)
+    def _():
+        out_ref[...] = cur_ref[...]
+
+
+def rest_kernel(axis, near_ref, across_ref, cur_ref, out_ref):
+    mine = lax.axis_index(axis)
+
+    @pl.when(mine >= 2)
+    def _():
+        out_ref[...] = cur_ref[...]
 
     @pl.when(mine < 2)
     def _():
-        second = jnp.concatenate([near_ref[0, N:], near_ref[1, N:]], axis=0)
-        out_ref[...] = mm(split(out_ref[...]), split(second))
+        second = jnp.concatenate([across_ref[0], across_ref[1]], axis=0)
+        out_ref[...] = mm(split(cur_ref[...]), split(second))
 
     @pl.when(mine < 1)
     def _():
-        out_ref[...] = mm(split(out_ref[...]), split(near_ref[1, :N]))
+        out_ref[...] = mm(split(out_ref[...]), split(near_ref[1]))
 
 
 VMEM = pl.BlockSpec(memory_space=pltpu.VMEM)
 
 
-def call(kernel, name, outs, args, products, scratch=(), space=VMEM, limit=VMEM_BYTES):
+def call(kernel, outs, args, products, scratch=(), space=VMEM, limit=VMEM_BYTES):
     many = isinstance(outs, list)
     shapes = [jax.ShapeDtypeStruct(s, F32) for s in (outs if many else [outs])]
     moved = sum(a.size * 4 for a in args) + sum(s.size * 4 for s in shapes)
     return pl.pallas_call(
         kernel,
-        name=name,
         out_shape=shapes if many else shapes[0],
         in_specs=[space] * len(args),
         out_specs=[VMEM] * len(shapes) if many else VMEM,
@@ -236,15 +256,14 @@
 
 
 ROW_ODD = from_later((1, 3))
-ROW_EVEN = from_later((2, 2))
-
-
-def shards(anomalies, mean_state, obs_rows, obs_precision):
+ROW_EVEN = [(row, row - 2) for row in range(2, 4)]
+
+
+def smoother(anomalies, mean_state, obs_rows, obs_precision):
     current = anomalies[0]
     sources = (current, mean_state, obs_rows, obs_precision)
     gram = call(
         gram_kernel,
-        "gram",
         (PACK, H),
         sources,
         1,
@@ -255,27 +274,33 @@
     both = lax.all_gather(gram, "core")
     spread = jnp.broadcast_to(both[0] + both[1], (4, PACK, H))
     parts = lax.all_to_all(spread, "x", 0, 0)
-    half = call(
-        root_kernel, "root", (4, PACK // 2, H), (parts,), 6, [pltpu.VMEM((PACK, H), F32)]
-    )
+    half = call(root_kernel, (4, PACK // 2, H), (parts,), 6, [pltpu.VMEM((PACK, H), F32)])
     parts = lax.all_gather(lax.all_to_all(half, "zl", 0, 0), "core")
     full = (N, N)
-    total, half = call(quad_kernel, "quad", [full, (H, N)], (parts,), 3)
-    current = call(quad_apply_kernel, "quad_apply", full, (parts, current), 4)
-    across = lax.ppermute(half, ("zh", "zl"), ACROSS)
-    near = lax.ppermute(total, ("zh", "zl", "core"), NEAR)
-    near = lax.all_gather(jnp.concatenate([near, across], axis=0), "core")
-    square = pltpu.VMEM(full, F32)
+    total, half = call(quad_kernel, [full, (H, N)], (parts,), 3)
+    current = call(quad_apply_kernel, full, (parts, current), 4)
+    near, across = exchange(total, half, ("zh", "zl"), NEAR, ACROSS)
+    beside = call(beside_kernel, full, (near, total), 1)
     total, half = call(
-        ring_kernel, "ring", [full, (H, N)], (near, total), 3, [square, square]
+        ring_kernel, [full, (H, N)], (near, across, beside), 2, [pltpu.VMEM(full, F32)]
     )
-    current = call(
-        functools.partial(apply_kernel, "zh"), "ring_apply", full, (near, current), 3
-    )
-    near = lax.ppermute(total, ("y", "core"), ROW_ODD)
-    half = lax.ppermute(half, ("y", "core"), ROW_EVEN)
-    near = lax.all_gather(jnp.concatenate([near, half], axis=0), "core")
-    return call(functools.partial(apply_kernel, "y"), "row_apply", full, (near, current), 3)[None]
+    current = apply(current, near, across, "zh")
+    near, across = exchange(total, half, ("y",), ROW_ODD, ROW_EVEN)
+    return apply(current, near, across, "y")[None]
+
+
+def exchange(total, half, axes, near_pairs, across_pairs):
+    near = lax.ppermute(total, (*axes, "core"), near_pairs)
+    across = lax.ppermute(half, axes, across_pairs)
+    near = lax.all_gather(near, "core")
+    return near, lax.all_gather(across, "core")
+
+
+def apply(current, near, across, axis):
+    first = functools.partial(first_kernel, axis)
+    rest = functools.partial(rest_kernel, axis)
+    current = call(first, (N, N), (near, current), 1)
+    return call(rest, (N, N), (near, across, current), 2)
 
 
 def solution(mesh):
@@ -284,5 +309,5 @@
     win, state = ("y", "zh", "zl"), ("x", "core")
     placed = (P(win, state, None), P(win, state), P(win, state), P(win, state))
     return jax.shard_map(
-        shards, mesh=grid, in_specs=placed, out_specs=P(win, state, None), check_vma=False
+        smoother, mesh=grid, in_specs=placed, out_specs=P(win, state, None), check_vma=False
     )

time: 92.9 us -> 96.2 us (1.036)
  blocking collectives: 39.6 us -> 44 us
  waiting for transfers between devices: 26.2 us -> 24.6 us
    all_gather x4 -> x6, blocking collectives: 18.2 us -> 22.6 us  [the longest x1 8.69 us: smoother(): both = lax.all_gather(gram, 'core')]
    ppermute x4, waiting for transfers between devices: 26.2 us -> 24.6 us  [the longest x2 24.6 us: exchange(): across = lax.ppermute(half, axes, across_pairs)]
    pallas_call x7 -> x10, Pallas kernels: 10 us -> 10.1 us  [call(): pl.pallas_call(kernel, out_shape=shapes if many else shapes[0], in_specs=...]
  transfers between devices with their start and end apart: 4 -> 4, of which waited for: 3 -> 2; matrix products, arithmetic and copies ran while one was open for 0% -> 0% of each run, Pallas kernels for 3% -> 2%
where the time goes in v4:
time: 96.2 us; the launch traced here: 95.5 us
  blocking collectives  44 us (46%)
  waiting for transfers between devices  24.6 us (26%)
  starting transfers between devices  16.5 us (17%)
  Pallas kernels  10.1 us (10%)
    ppermute x2, waiting for transfers between devices, exchange(): across = lax.ppermute(half, axes, across_pairs)  24.6 us
    all_to_all x1, blocking collectives, smoother(): parts = lax.all_to_all(spread, 'x', 0, 0)  11.8 us
    pallas_call x10, Pallas kernels, call(): pl.pallas_call(kernel, out_shape=shapes if many else shapes[0], in_specs=...  10.1 us
    all_to_all x1, blocking collectives, smoother(): parts = lax.all_gather(lax.all_to_all(half, 'zl', 0, 0), 'core')  9.56 us
    ppermute x2, starting transfers between devices, exchange(): near = lax.ppermute(total, (*axes, 'core'), near_pairs)  9.09 us
    all_gather x1, blocking collectives, smoother(): both = lax.all_gather(gram, 'core')  8.69 us
    ppermute x2, starting transfers between devices, exchange(): across = lax.ppermute(half, axes, across_pairs)  7.43 us
    all_gather x1, blocking collectives, smoother(): parts = lax.all_gather(lax.all_to_all(half, 'zl', 0, 0), 'core')  4.8 us
  transfers between devices with their start and end apart: 4, of which 2 were waited for; matrix products, arithmetic and copies ran while one was open for 0% of the time, Pallas kernels for 2%

profile of v4, /device:TPU:1, one launch (start us, length us, event | category | flops | bytes accessed | tf_op | source)
XLA Modules:
  0.0 95.5 jit_solution(16664673268914326294)
XLA Ops:
  0.0 2.4 %shard_map.46 = f32[272,128]{1,0:T(8,128)} custom-call(f32[256,256]{1,0:T(8,128)} %bitcast.18, f32[1,256]{1,0:T(1,128)} %refs_1_.1, s32[1,128]{1,0:T(1,128)} %refs_2_.1, f32[1,128]{1,0:T(1,128)} %refs_3_.1), custom_call_target="tpu_custom_call" | custom-call | flops 100663296 | bytes 403456 | tf_op jit(solution)/shard_map/pallas_call | solution.py:228
  2.5 8.7 %all-gather = f32[544,128]{1,0:T(8,128)S(1)} all-gather(f32[272,128]{1,0:T(8,128)} %shard_map.46), channel_id=2, replica_groups=mesh['y'=4,'zh'=4,'zl'=4,'x'=4,'core'=2] {'core'}, dimensions={0}, use_global_device_ids=true | all-gather | bytes 417792 | tf_op jit(solution)/shard_map/all_gather | solution.py:274
  11.2 11.8 %all_to_all.10.parts_ref = f32[4,272,128]{2,1,0:T(8,128)S(1)} all-to-all(f32[4,272,128]{2,1,0:T(8,128)S(1)} %broadcast_in_dim.6), channel_id=1, replica_groups=mesh['y'=4,'zh'=4,'zl'=4,'x'=4,'core'=2] {'x'}, dimensions={0} | all-to-all | bytes 1114112 | tf_op jit(solution)/shard_map/all_to_all | solution.py:276
  23.0 1.9 %shard_map.47 = f32[4,136,128]{2,1,0:T(8,128)S(1)} custom-call(f32[4,272,128]{2,1,0:T(8,128)S(1)} %all_to_all.10.parts_ref), custom_call_target="tpu_custom_call" | custom-call | flops 603979776 | bytes 835584 | tf_op jit(solution)/shard_map/pallas_call | solution.py:228
  25.0 9.6 %all_to_all.11 = f32[4,136,128]{2,1,0:T(8,128)S(1)} all-to-all(f32[4,136,128]{2,1,0:T(8,128)S(1)} %shard_map.47), channel_id=1, replica_groups=mesh['y'=4,'zh'=4,'zl'=4,'x'=4,'core'=2] {'zl'}, dimensions={0} | all-to-all | bytes 557056 | tf_op jit(solution)/shard_map/all_to_all | solution.py:278
  34.5 4.8 %all-gather.1 = f32[8,136,128]{2,1,0:T(8,128)S(1)} all-gather(f32[4,136,128]{2,1,0:T(8,128)S(1)} %all_to_all.11), channel_id=3, replica_groups=mesh['y'=4,'zh'=4,'zl'=4,'x'=4,'core'=2] {'core'}, dimensions={0}, use_global_device_ids=true | all-gather | bytes 835584 | tf_op jit(solution)/shard_map/all_gather | solution.py:278
  39.3 0.9 shard_map.48
  40.3 7.8 %collective-permute-start = (f32[256,256]{1,0:T(8,128)S(1)}, f32[256,256]{1,0:T(8,128)S(1)}, u32[]{:S(2)}, u32[]{:S(2)}) collective-permute-start(f32[256,256]{1,0:T(8,128)S(1)} %get-tuple-element.9.mine_ref), channel_id=1, source_target_pairs={{0,96},{8,104},{16,112},{24,120},{32,0},{40,8},{48,16},{56,24},{64... | collective-permute-start | bytes 786440 | tf_op jit(solution)/shard_map/ppermute | solution.py:293
  48.1 6.1 %collective-permute-start.1 = (f32[128,256]{1,0:T(8,128)S(1)}, f32[128,256]{1,0:T(8,128)S(1)}, u32[]{:S(2)}, u32[]{:S(2)}) collective-permute-start(f32[128,256]{1,0:T(8,128)S(1)} %get-tuple-element.10), channel_id=1, source_target_pairs={{0,88},{8,80},{16,72},{24,64},{32,120},{40,112},{48,104},{56,96},{... | collective-permute-start | bytes 393224 | tf_op jit(solution)/shard_map/ppermute | solution.py:294
  54.2 20.0 %collective-permute-done.1 = f32[128,256]{1,0:T(8,128)S(1)} collective-permute-done((f32[128,256]{1,0:T(8,128)S(1)}, f32[128,256]{1,0:T(8,128)S(1)}, u32[]{:S(2)}, u32[]{:S(2)}) %collective-permute-start.1) | collective-permute-done | bytes 131104 | tf_op jit(solution)/shard_map/ppermute | solution.py:294
  74.2 2.0 %all-gather.3 = f32[256,256]{1,0:T(8,128)S(1)} all-gather(f32[128,256]{1,0:T(8,128)S(1)} %collective-permute-done.1), channel_id=5, replica_groups=mesh['y'=4,'zh'=4,'zl'=4,'x'=4,'core'=2] {'core'}, dimensions={0}, use_global_device_ids=true | all-gather | bytes 393216 | tf_op jit(solution)/shard_map/all_gather | solution.py:296
  76.2 0.0 collective-permute-done
  76.2 2.2 %all-gather.2 = f32[512,256]{1,0:T(8,128)S(1)} all-gather(f32[256,256]{1,0:T(8,128)S(1)} %collective-permute-done), channel_id=4, replica_groups=mesh['y'=4,'zh'=4,'zl'=4,'x'=4,'core'=2] {'core'}, dimensions={0}, use_global_device_ids=true | all-gather | bytes 786432 | tf_op jit(solution)/shard_map/all_gather | solution.py:295
  78.4 0.3 shard_map.49.beside_ref
  78.7 0.0 copy-start
  78.7 0.7 shard_map.50
  79.4 1.3 %collective-permute-start.2 = (f32[256,256]{1,0:T(8,128)S(1)}, f32[256,256]{1,0:T(8,128)S(1)}, u32[]{:S(2)}, u32[]{:S(2)}) collective-permute-start(f32[256,256]{1,0:T(8,128)S(1)} %get-tuple-element.11), channel_id=1, source_target_pairs={{128,0},{256,128},{384,256},{385,1},{130,2},{258,130},{386,258},{3... | collective-permute-start | bytes 786440 | tf_op jit(solution)/shard_map/ppermute | solution.py:293
  80.7 1.3 %collective-permute-start.3 = (f32[128,256]{1,0:T(8,128)S(1)}, f32[128,256]{1,0:T(8,128)S(1)}, u32[]{:S(2)}, u32[]{:S(2)}) collective-permute-start(f32[128,256]{1,0:T(8,128)S(1)} %get-tuple-element.12), channel_id=1, source_target_pairs={{256,0},{384,128},{257,1},{385,129},{258,2},{386,130},{259,3},{387... | collective-permute-start | bytes 393224 | tf_op jit(solution)/shard_map/ppermute | solution.py:294
  82.0 0.0 copy-done
  82.0 1.5 %shard_map.51.cur_ref = f32[256,256]{1,0:T(8,128)S(1)} custom-call(f32[2,4,136,128]{3,2,1,0:T(8,128)S(1)} %bitcast.17, f32[256,256]{1,0:T(8,128)S(1)} %bitcast.19), custom_call_target="tpu_custom_call" | custom-call | flops 402653184 | bytes 1081344 | tf_op jit(solution)/shard_map/pallas_call | solution.py:228
  83.5 0.3 shard_map.52.cur_ref
  83.8 0.6 shard_map.53.cur_ref
  84.3 4.6 %collective-permute-done.3 = f32[128,256]{1,0:T(8,128)S(1)} collective-permute-done((f32[128,256]{1,0:T(8,128)S(1)}, f32[128,256]{1,0:T(8,128)S(1)}, u32[]{:S(2)}, u32[]{:S(2)}) %collective-permute-start.3) | collective-permute-done | bytes 131104 | tf_op jit(solution)/shard_map/ppermute | solution.py:294
  88.9 2.8 %all-gather.5 = f32[256,256]{1,0:T(8,128)S(1)} all-gather(f32[128,256]{1,0:T(8,128)S(1)} %collective-permute-done.3), channel_id=7, replica_groups=mesh['y'=4,'zh'=4,'zl'=4,'x'=4,'core'=2] {'core'}, dimensions={0}, use_global_device_ids=true | all-gather | bytes 393216 | tf_op jit(solution)/shard_map/all_gather | solution.py:296
  91.7 0.0 collective-permute-done.2
  91.7 2.2 %all-gather.4 = f32[512,256]{1,0:T(8,128)S(1)} all-gather(f32[256,256]{1,0:T(8,128)S(1)} %collective-permute-done.2), channel_id=6, replica_groups=mesh['y'=4,'zh'=4,'zl'=4,'x'=4,'core'=2] {'core'}, dimensions={0}, use_global_device_ids=true | all-gather | bytes 786432 | tf_op jit(solution)/shard_map/all_gather | solution.py:295
  93.9 0.3 shard_map.54.cur_ref
  94.2 1.3 %shard_map.55 = f32[256,256]{1,0:T(8,128)} custom-call(f32[2,256,256]{2,1,0:T(8,128)S(1)} %bitcast.12, f32[2,128,256]{2,1,0:T(8,128)S(1)} %bitcast.15, f32[256,256]{1,0:T(8,128)S(1)} %shard_map.54.cur_ref), custom_call_target="tpu_custom_call" | custom-call | flops 201326592 | bytes 1310720 | tf_op jit(solution)/shard_map/pallas_call | solution.py:228
  (2 shorter events, 0.1 us)
Async XLA Ops:
  40.3 36.0 %collective-permute-start = (f32[256,256]{1,0:T(8,128)S(1)}, f32[256,256]{1,0:T(8,128)S(1)}, u32[]{:S(2)}, u32[]{:S(2)}) collective-permute-start(f32[256,256]{1,0:T(8,128)S(1)} %get-tuple-element.9.mine_ref), channel_id=1, source_target_pairs={{0,96},{8,104},{16,112},{24,120},{32,0},{40,8},{48,16},{56,24},{64... | collective-permute-start | bytes 786440 | tf_op jit(solution)/shard_map/ppermute | solution.py:293
  48.1 26.2 %collective-permute-start.1 = (f32[128,256]{1,0:T(8,128)S(1)}, f32[128,256]{1,0:T(8,128)S(1)}, u32[]{:S(2)}, u32[]{:S(2)}) collective-permute-start(f32[128,256]{1,0:T(8,128)S(1)} %get-tuple-element.10), channel_id=1, source_target_pairs={{0,88},{8,80},{16,72},{24,64},{32,120},{40,112},{48,104},{56,96},{... | collective-permute-start | bytes 393224 | tf_op jit(solution)/shard_map/ppermute | solution.py:294
  78.7 3.3 %copy-start = (f32[1,256,256]{2,1,0:T(8,128)S(1)}, f32[1,256,256]{2,1,0:T(8,128)}, u32[]{:S(2)}) copy-start(f32[1,256,256]{2,1,0:T(8,128)} %param.4) | copy-start | bytes 786436
  79.4 12.3 %collective-permute-start.2 = (f32[256,256]{1,0:T(8,128)S(1)}, f32[256,256]{1,0:T(8,128)S(1)}, u32[]{:S(2)}, u32[]{:S(2)}) collective-permute-start(f32[256,256]{1,0:T(8,128)S(1)} %get-tuple-element.11), channel_id=1, source_target_pairs={{128,0},{256,128},{384,256},{385,1},{130,2},{258,130},{386,258},{3... | collective-permute-start | bytes 786440 | tf_op jit(solution)/shard_map/ppermute | solution.py:293
  80.7 8.2 %collective-permute-start.3 = (f32[128,256]{1,0:T(8,128)S(1)}, f32[128,256]{1,0:T(8,128)S(1)}, u32[]{:S(2)}, u32[]{:S(2)}) collective-permute-start(f32[128,256]{1,0:T(8,128)S(1)} %get-tuple-element.12), channel_id=1, source_target_pairs={{256,0},{384,128},{257,1},{385,129},{258,2},{386,130},{259,3},{387... | collective-permute-start | bytes 393224 | tf_op jit(solution)/shard_map/ppermute | solution.py:294

commit v5 on v4

--- a/solution.py
+++ b/solution.py
@@ -14,7 +14,6 @@
 H = 128
 PACK = 272
 NS_STEPS = 3
-ALL_VMEM = 67043328
 VMEM_BYTES = 8 * 1024 * 1024
 
 
@@ -189,33 +188,40 @@
     half_ref[...] = total_ref[pl.ds(pl.multiple_of(core * H, 8), H), :]
 
 
-def first_kernel(axis, near_ref, cur_ref, out_ref):
-    mine = lax.axis_index(axis)
-
-    @pl.when(mine < 3)
-    def _():
-        out_ref[...] = mm(split(cur_ref[...]), split(near_ref[0]))
-
-    @pl.when(mine == 3)
-    def _():
-        out_ref[...] = cur_ref[...]
-
-
-def rest_kernel(axis, near_ref, across_ref, cur_ref, out_ref):
-    mine = lax.axis_index(axis)
-
-    @pl.when(mine >= 2)
-    def _():
-        out_ref[...] = cur_ref[...]
-
-    @pl.when(mine < 2)
+def ring_apply_kernel(near_ref, across_ref, cur_ref, out_ref):
+    quad = lax.axis_index("zh")
+    out_ref[...] = cur_ref[...]
+
+    @pl.when(quad < 3)
+    def _():
+        out_ref[...] = mm(split(out_ref[...]), split(near_ref[0]))
+
+    @pl.when(quad < 2)
     def _():
         second = jnp.concatenate([across_ref[0], across_ref[1]], axis=0)
-        out_ref[...] = mm(split(cur_ref[...]), split(second))
-
-    @pl.when(mine < 1)
+        out_ref[...] = mm(split(out_ref[...]), split(second))
+
+    @pl.when(quad < 1)
     def _():
         out_ref[...] = mm(split(out_ref[...]), split(near_ref[1]))
+
+
+def row_apply_kernel(near_ref, cur_ref, out_ref):
+    row = lax.axis_index("y")
+    out_ref[...] = cur_ref[...]
+
+    @pl.when(row < 3)
+    def _():
+        out_ref[...] = mm(split(out_ref[...]), split(near_ref[0, :N]))
+
+    @pl.when(row < 2)
+    def _():
+        second = jnp.concatenate([near_ref[0, N:], near_ref[1, N:]], axis=0)
+        out_ref[...] = mm(split(out_ref[...]), split(second))
+
+    @pl.when(row < 1)
+    def _():
+        out_ref[...] = mm(split(out_ref[...]), split(near_ref[1, :N]))
 
 
 VMEM = pl.BlockSpec(memory_space=pltpu.VMEM)
@@ -265,11 +271,10 @@
     gram = call(
         gram_kernel,
         (PACK, H),
-        sources,
+        [pltpu.with_memory_space_constraint(a, pltpu.HBM) for a in sources],
         1,
         [pltpu.VMEM(a.shape, a.dtype) for a in sources] + [pltpu.SemaphoreType.DMA((4,))],
         pl.BlockSpec(memory_space=pltpu.HBM),
-        ALL_VMEM - PACK * H * 4,
     )
     both = lax.all_gather(gram, "core")
     spread = jnp.broadcast_to(both[0] + both[1], (4, PACK, H))
@@ -279,28 +284,19 @@
     full = (N, N)
     total, half = call(quad_kernel, [full, (H, N)], (parts,), 3)
     current = call(quad_apply_kernel, full, (parts, current), 4)
-    near, across = exchange(total, half, ("zh", "zl"), NEAR, ACROSS)
+    near = lax.ppermute(total, ("zh", "zl", "core"), NEAR)
+    across = lax.ppermute(half, ("zh", "zl"), ACROSS)
+    near = lax.all_gather(near, "core")
+    across = lax.all_gather(across, "core")
     beside = call(beside_kernel, full, (near, total), 1)
     total, half = call(
         ring_kernel, [full, (H, N)], (near, across, beside), 2, [pltpu.VMEM(full, F32)]
     )
-    current = apply(current, near, across, "zh")
-    near, across = exchange(total, half, ("y",), ROW_ODD, ROW_EVEN)
-    return apply(current, near, across, "y")[None]
-
-
-def exchange(total, half, axes, near_pairs, across_pairs):
-    near = lax.ppermute(total, (*axes, "core"), near_pairs)
-    across = lax.ppermute(half, axes, across_pairs)
-    near = lax.all_gather(near, "core")
-    return near, lax.all_gather(across, "core")
-
-
-def apply(current, near, across, axis):
-    first = functools.partial(first_kernel, axis)
-    rest = functools.partial(rest_kernel, axis)
-    current = call(first, (N, N), (near, current), 1)
-    return call(rest, (N, N), (near, across, current), 2)
+    current = call(ring_apply_kernel, full, (near, across, current), 3)
+    near = lax.ppermute(total, ("y", "core"), ROW_ODD)
+    across = lax.ppermute(half, "y", ROW_EVEN)
+    near = lax.all_gather(jnp.concatenate([near, across], axis=0), "core")
+    return call(row_apply_kernel, full, (near, current), 3)[None]
 
 
 def solution(mesh):

time: 96.2 us -> 93.9 us (0.976)
  blocking collectives: 44 us -> 41.2 us
  waiting for transfers between devices: 24.6 us -> 26.2 us
    all_gather x4 -> x3, blocking collectives: 9.11 us -> 6.52 us  [the longest x1 2.37 us: smoother(): near = lax.all_gather(jnp.concatenate([near, across], axis=0), 'core')]
    ppermute x4, waiting for transfers between devices: 24.6 us -> 26.2 us  [the longest x1 20 us: smoother(): across = lax.ppermute(half, ('zh', 'zl'), ACROSS)]
    pallas_call x10 -> x8, Pallas kernels: 10.1 us -> 9.48 us  [call(): pl.pallas_call(kernel, out_shape=shapes if many else shapes[0], in_specs=...]
  transfers between devices with their start and end apart: 4 -> 4, of which waited for: 2 -> 3; matrix products, arithmetic and copies ran while one was open for 0% -> 0% of each run, Pallas kernels for 2% -> 2%
where the time goes in v5:
time: 93.9 us; the launch traced here: 93.6 us
  blocking collectives  41.2 us (44%)
  waiting for transfers between devices  26.2 us (28%)
  starting transfers between devices  16.5 us (18%)
  Pallas kernels  9.48 us (10%)
    ppermute x1, waiting for transfers between devices, smoother(): across = lax.ppermute(half, ('zh', 'zl'), ACROSS)  20 us
    all_to_all x1, blocking collectives, smoother(): parts = lax.all_to_all(spread, 'x', 0, 0)  11.8 us
    all_to_all x1, blocking collectives, smoother(): parts = lax.all_gather(lax.all_to_all(half, 'zl', 0, 0), 'core')  9.56 us
    pallas_call x8, Pallas kernels, call(): pl.pallas_call(kernel, out_shape=shapes if many else shapes[0], in_specs=...  9.48 us
    all_gather x1, blocking collectives, smoother(): both = lax.all_gather(gram, 'core')  8.48 us
    ppermute x1, starting transfers between devices, smoother(): near = lax.ppermute(total, ('zh', 'zl', 'core'), NEAR)  7.8 us
    ppermute x1, starting transfers between devices, smoother(): across = lax.ppermute(half, ('zh', 'zl'), ACROSS)  6.13 us
    all_gather x1, blocking collectives, smoother(): parts = lax.all_gather(lax.all_to_all(half, 'zl', 0, 0), 'core')  4.8 us
  transfers between devices with their start and end apart: 4, of which 3 were waited for; matrix products, arithmetic and copies ran while one was open for 0% of the time, Pallas kernels for 2%

profile of v5, /device:TPU:1, one launch (start us, length us, event | category | flops | bytes accessed | tf_op | source)
XLA Modules:
  0.0 93.6 jit_solution(4667422271355260179)
XLA Ops:
  0.0 1.8 %shard_map.46 = f32[272,128]{1,0:T(8,128)S(1)} custom-call(f32[256,256]{1,0:T(8,128)} %bitcast.14, f32[1,256]{1,0:T(1,128)} %refs_1_.1, s32[1,128]{1,0:T(1,128)} %refs_2_.1, f32[1,128]{1,0:T(1,128)} %refs_3_.1), custom_call_target="tpu_custom_call" | custom-call | flops 100663296 | bytes 403456 | tf_op jit(solution)/shard_map/pallas_call | solution.py:234
  1.8 8.5 %all-gather = f32[544,128]{1,0:T(8,128)S(1)} all-gather(f32[272,128]{1,0:T(8,128)S(1)} %shard_map.46), channel_id=2, replica_groups=mesh['y'=4,'zh'=4,'zl'=4,'x'=4,'core'=2] {'core'}, dimensions={0}, use_global_device_ids=true | all-gather | bytes 417792 | tf_op jit(solution)/shard_map/all_gather | solution.py:279
  10.3 11.8 %all_to_all.10.parts_ref = f32[4,272,128]{2,1,0:T(8,128)S(1)} all-to-all(f32[4,272,128]{2,1,0:T(8,128)S(1)} %broadcast_in_dim.6), channel_id=1, replica_groups=mesh['y'=4,'zh'=4,'zl'=4,'x'=4,'core'=2] {'x'}, dimensions={0} | all-to-all | bytes 1114112 | tf_op jit(solution)/shard_map/all_to_all | solution.py:281
  22.2 1.9 %shard_map.47 = f32[4,136,128]{2,1,0:T(8,128)S(1)} custom-call(f32[4,272,128]{2,1,0:T(8,128)S(1)} %all_to_all.10.parts_ref), custom_call_target="tpu_custom_call" | custom-call | flops 603979776 | bytes 835584 | tf_op jit(solution)/shard_map/pallas_call | solution.py:234
  24.1 9.6 %all_to_all.11 = f32[4,136,128]{2,1,0:T(8,128)S(1)} all-to-all(f32[4,136,128]{2,1,0:T(8,128)S(1)} %shard_map.47), channel_id=1, replica_groups=mesh['y'=4,'zh'=4,'zl'=4,'x'=4,'core'=2] {'zl'}, dimensions={0} | all-to-all | bytes 557056 | tf_op jit(solution)/shard_map/all_to_all | solution.py:283
  33.7 4.8 %all-gather.1 = f32[8,136,128]{2,1,0:T(8,128)S(1)} all-gather(f32[4,136,128]{2,1,0:T(8,128)S(1)} %all_to_all.11), channel_id=3, replica_groups=mesh['y'=4,'zh'=4,'zl'=4,'x'=4,'core'=2] {'core'}, dimensions={0}, use_global_device_ids=true | all-gather | bytes 835584 | tf_op jit(solution)/shard_map/all_gather | solution.py:283
  38.5 0.9 shard_map.48
  39.4 7.8 %collective-permute-start = (f32[256,256]{1,0:T(8,128)S(1)}, f32[256,256]{1,0:T(8,128)S(1)}, u32[]{:S(2)}, u32[]{:S(2)}) collective-permute-start(f32[256,256]{1,0:T(8,128)S(1)} %get-tuple-element.9.mine_ref), channel_id=1, source_target_pairs={{0,96},{8,104},{16,112},{24,120},{32,0},{40,8},{48,16},{56,24},{64... | collective-permute-start | bytes 786440 | tf_op jit(solution)/shard_map/ppermute | solution.py:287
  47.2 6.1 %collective-permute-start.1 = (f32[128,256]{1,0:T(8,128)S(1)}, f32[128,256]{1,0:T(8,128)S(1)}, u32[]{:S(2)}, u32[]{:S(2)}) collective-permute-start(f32[128,256]{1,0:T(8,128)S(1)} %get-tuple-element.10), channel_id=1, source_target_pairs={{0,88},{8,80},{16,72},{24,64},{32,120},{40,112},{48,104},{56,96},{... | collective-permute-start | bytes 393224 | tf_op jit(solution)/shard_map/ppermute | solution.py:288
  53.3 20.0 %collective-permute-done.1 = f32[128,256]{1,0:T(8,128)S(1)} collective-permute-done((f32[128,256]{1,0:T(8,128)S(1)}, f32[128,256]{1,0:T(8,128)S(1)}, u32[]{:S(2)}, u32[]{:S(2)}) %collective-permute-start.1) | collective-permute-done | bytes 131104 | tf_op jit(solution)/shard_map/ppermute | solution.py:288
  73.4 2.0 %all-gather.3 = f32[256,256]{1,0:T(8,128)S(1)} all-gather(f32[128,256]{1,0:T(8,128)S(1)} %collective-permute-done.1), channel_id=5, replica_groups=mesh['y'=4,'zh'=4,'zl'=4,'x'=4,'core'=2] {'core'}, dimensions={0}, use_global_device_ids=true | all-gather | bytes 393216 | tf_op jit(solution)/shard_map/all_gather | solution.py:290
  75.4 0.0 collective-permute-done
  75.4 2.2 %all-gather.2 = f32[512,256]{1,0:T(8,128)S(1)} all-gather(f32[256,256]{1,0:T(8,128)S(1)} %collective-permute-done), channel_id=4, replica_groups=mesh['y'=4,'zh'=4,'zl'=4,'x'=4,'core'=2] {'core'}, dimensions={0}, use_global_device_ids=true | all-gather | bytes 786432 | tf_op jit(solution)/shard_map/all_gather | solution.py:289
  77.5 0.3 shard_map.49.beside_ref
  77.8 0.0 copy-start
  77.9 0.6 shard_map.50
  78.5 1.3 %collective-permute-start.2 = (f32[256,256]{1,0:T(8,128)S(1)}, f32[256,256]{1,0:T(8,128)S(1)}, u32[]{:S(2)}, u32[]{:S(2)}) collective-permute-start(f32[256,256]{1,0:T(8,128)S(1)} %get-tuple-element.11), channel_id=1, source_target_pairs={{128,0},{256,128},{384,256},{385,1},{130,2},{258,130},{386,258},{3... | collective-permute-start | bytes 786440 | tf_op jit(solution)/shard_map/ppermute | solution.py:296
  79.8 1.3 %collective-permute-start.3 = (f32[128,256]{1,0:T(8,128)S(1)}, f32[128,256]{1,0:T(8,128)S(1)}, u32[]{:S(2)}, u32[]{:S(2)}) collective-permute-start(f32[128,256]{1,0:T(8,128)S(1)} %get-tuple-element.12), channel_id=1, source_target_pairs={{256,0},{384,128},{257,1},{385,129},{258,2},{386,130},{259,3},{387... | collective-permute-start | bytes 393224 | tf_op jit(solution)/shard_map/ppermute | solution.py:297
  81.1 0.0 copy-done
  81.1 1.5 %shard_map.51.cur_ref = f32[256,256]{1,0:T(8,128)S(1)} custom-call(f32[2,4,136,128]{3,2,1,0:T(8,128)S(1)} %bitcast.13, f32[256,256]{1,0:T(8,128)S(1)} %bitcast.15), custom_call_target="tpu_custom_call" | custom-call | flops 402653184 | bytes 1081344 | tf_op jit(solution)/shard_map/pallas_call | solution.py:234
  82.6 0.9 shard_map.52.cur_ref
  83.5 4.6 %collective-permute-done.3 = f32[128,256]{1,0:T(8,128)S(1)} collective-permute-done((f32[128,256]{1,0:T(8,128)S(1)}, f32[128,256]{1,0:T(8,128)S(1)}, u32[]{:S(2)}, u32[]{:S(2)}) %collective-permute-start.3) | collective-permute-done | bytes 131104 | tf_op jit(solution)/shard_map/ppermute | solution.py:297
  88.1 1.6 %collective-permute-done.2 = f32[256,256]{1,0:T(8,128)S(1)} collective-permute-done((f32[256,256]{1,0:T(8,128)S(1)}, f32[256,256]{1,0:T(8,128)S(1)}, u32[]{:S(2)}, u32[]{:S(2)}) %collective-permute-start.2) | collective-permute-done | bytes 262176 | tf_op jit(solution)/shard_map/ppermute | solution.py:296
  89.7 2.4 %all-gather.4 = f32[768,256]{1,0:T(8,128)S(1)} all-gather(f32[384,256]{1,0:T(8,128)S(1)} %pad_maximum_fusion), channel_id=6, replica_groups=mesh['y'=4,'zh'=4,'zl'=4,'x'=4,'core'=2] {'core'}, dimensions={0}, use_global_device_ids=true | all-gather | bytes 1179648 | tf_op jit(solution)/shard_map/all_gather | solution.py:298
  92.1 1.6 %shard_map.53 = f32[256,256]{1,0:T(8,128)} custom-call(f32[2,384,256]{2,1,0:T(8,128)S(1)} %bitcast.9, f32[256,256]{1,0:T(8,128)S(1)} %shard_map.52.cur_ref), custom_call_target="tpu_custom_call" | custom-call | flops 301989888 | bytes 1310720 | tf_op jit(solution)/shard_map/pallas_call | solution.py:234
  (3 shorter events, 0.1 us)
Async XLA Ops:
  39.4 36.0 %collective-permute-start = (f32[256,256]{1,0:T(8,128)S(1)}, f32[256,256]{1,0:T(8,128)S(1)}, u32[]{:S(2)}, u32[]{:S(2)}) collective-permute-start(f32[256,256]{1,0:T(8,128)S(1)} %get-tuple-element.9.mine_ref), channel_id=1, source_target_pairs={{0,96},{8,104},{16,112},{24,120},{32,0},{40,8},{48,16},{56,24},{64... | collective-permute-start | bytes 786440 | tf_op jit(solution)/shard_map/ppermute | solution.py:287
  47.2 26.2 %collective-permute-start.1 = (f32[128,256]{1,0:T(8,128)S(1)}, f32[128,256]{1,0:T(8,128)S(1)}, u32[]{:S(2)}, u32[]{:S(2)}) collective-permute-start(f32[128,256]{1,0:T(8,128)S(1)} %get-tuple-element.10), channel_id=1, source_target_pairs={{0,88},{8,80},{16,72},{24,64},{32,120},{40,112},{48,104},{56,96},{... | collective-permute-start | bytes 393224 | tf_op jit(solution)/shard_map/ppermute | solution.py:288
  77.8 3.3 %copy-start = (f32[1,256,256]{2,1,0:T(8,128)S(1)}, f32[1,256,256]{2,1,0:T(8,128)}, u32[]{:S(2)}) copy-start(f32[1,256,256]{2,1,0:T(8,128)} %param.4) | copy-start | bytes 786436
  78.5 11.1 %collective-permute-start.2 = (f32[256,256]{1,0:T(8,128)S(1)}, f32[256,256]{1,0:T(8,128)S(1)}, u32[]{:S(2)}, u32[]{:S(2)}) collective-permute-start(f32[256,256]{1,0:T(8,128)S(1)} %get-tuple-element.11), channel_id=1, source_target_pairs={{128,0},{256,128},{384,256},{385,1},{130,2},{258,130},{386,258},{3... | collective-permute-start | bytes 786440 | tf_op jit(solution)/shard_map/ppermute | solution.py:296
  79.8 8.2 %collective-permute-start.3 = (f32[128,256]{1,0:T(8,128)S(1)}, f32[128,256]{1,0:T(8,128)S(1)}, u32[]{:S(2)}, u32[]{:S(2)}) collective-permute-start(f32[128,256]{1,0:T(8,128)S(1)} %get-tuple-element.12), channel_id=1, source_target_pairs={{256,0},{384,128},{257,1},{385,129},{258,2},{386,130},{259,3},{387... | collective-permute-start | bytes 393224 | tf_op jit(solution)/shard_map/ppermute | solution.py:297
